TPU v7x, 32 devices: a whole 2x2x4 slice. The times are simulated.
32 devices in a mesh: row: 8 (over y, x, core), col: 4 (over z).
Axes of the slice: x: 2, y: 2, z: 4, core: 2. Of those that a mesh axis runs over, the one named last changes fastest.
Arguments:
- rhs: float32 [32, 1024, 4096], P(None, 'row', 'col'), may hold values from -6 to 6
- factor: bfloat16 [32, 1024, 4, 1024], P(None, 'row', None, 'col'), may hold values from -0.09375 to 0.09375
- diag_inverse: bfloat16 [4, 1024, 1024], P(None, 'row'), may hold values from -1.5 to 1.5, as said below
Outputs:
- solution: float32 [4, 1024, 4096], P(None, 'row', 'col')
- remaining: float32 [28, 1024, 4096], P(None, 'row', 'col')
Inputs may be any that keep to these rules, and one draw needn't show every extreme that they name: Each diag_inverse[k] is lower triangular with diagonal entries from 0.5 to 1.5.
All inputs are finite; a program needn't handle non-finite values.
Results may differ from a plain program's by a relative error of at most 0.0044.
Values may be sent and summed in bfloat16 or wider, within the bound.
A program may use at most 192 MiB of HBM per device.

v0:
```python
import jax
import jax.numpy as jnp
from jax import lax
from jax.sharding import PartitionSpec as P

STEPS = 4


def shards(rhs, factor, diag_inverse):
    block_count, tile_rows, rhs_width = rhs.shape
    panel_cols = factor.shape[3]
    remaining_rows = rhs
    solved_list = []
    for section in range(STEPS):
        current = remaining_rows[0].astype(jnp.bfloat16)
        inverse_section = diag_inverse[section]
        own_rows = jnp.dot(
            inverse_section,
            lax.all_gather(current, "row", axis=0, tiled=True),
            preferred_element_type=jnp.float32,
        )
        whole_solved = lax.all_gather(own_rows.astype(jnp.bfloat16), "row", axis=0, tiled=True)
        solved_list.append(own_rows)
        later_count = block_count - section - 1
        lower_tiles = factor[section + 1 :, :, section, :]
        flat_tiles = lower_tiles.reshape(later_count * tile_rows, panel_cols)
        update = jnp.dot(
            lax.all_gather(flat_tiles, "col", axis=1, tiled=True),
            whole_solved,
            preferred_element_type=jnp.float32,
        )
        remaining_rows = remaining_rows[1:] - update.reshape(later_count, tile_rows, rhs_width)
    return (jnp.stack(solved_list), remaining_rows)


def solution(mesh):
    in_specs = (P(None, "row", "col"), P(None, "row", None, "col"), P(None, "row", None))
    out_specs = (P(None, "row", "col"), P(None, "row", "col"))
    return jax.shard_map(shards, mesh=mesh, in_specs=in_specs, out_specs=out_specs, check_vma=False)
```

profile of v0, /device:TPU:0, one launch (start us, length us, event | category | flops | bytes accessed | tf_op | source)
XLA Modules:
  0.0 999.6 jit_solution(11575915859656223268)
XLA Ops:
  9.1 32.0 %all-gather.33.cloned.1.call-done = bf16[1,1024,1024]{2,1,0:T(8,128)(2,1)} async-done(((bf16[1,128,1024]{2,1,0:T(8,128)(2,1)}), bf16[1,1024,1024]{2,1,0:T(8,128)(2,1)}) %all-gather.33.cloned.1.call-update) | async-done | bytes 2097168 | tf_op jit(solution)/shard_map/all_gather | solution.py:19
  56.8 15.2 %all-gather.17.cloned.1.call-done = bf16[1024,1024]{1,0:T(8,128)(2,1)} async-done(((bf16[128,1024]{1,0:T(8,128)(2,1)}), bf16[1024,1024]{1,0:T(8,128)(2,1)}) %all-gather.17.cloned.1.call-update) | async-done | bytes 2097168 | tf_op jit(solution)/shard_map/all_gather | solution.py:22
  72.0 147.0 %all-gather.19.cloned.1.call-done = bf16[3968,1024]{1,0:T(8,128)(2,1)} async-done(((bf16[3968,256]{1,0:T(8,128)(2,1)}), bf16[3968,1024]{1,0:T(8,128)(2,1)}) %all-gather.19.cloned.1.call-update) | async-done | bytes 8126480 | tf_op jit(solution)/shard_map/all_gather | solution.py:28
  219.0 15.9 %convolution_bitcast_fusion.3 = f32[3968,1024]{0,1:T(8,128)} fusion(bf16[1024,1024]{1,0:T(8,128)(2,1)} %all-gather.17.cloned.1.call-done, bf16[3968,1024]{1,0:T(8,128)(2,1)} %all-gather.19.cloned.1.call-done), kind=kOutput, calls=%fused_computation.7 | convolution fusion | flops 8321499136 | bytes 26476544 | tf_op jit(solution)/shard_map/dot_general | solution.py:27
  234.9 16.7 %copy.13 = f32[3968,1024]{1,0:T(8,128)} copy(f32[3968,1024]{0,1:T(8,128)} %convolution_bitcast_fusion.3) | data formatting | bytes 32505856 | tf_op jit(solution)/shard_map/dot_general | solution.py:27
  251.7 11.5 %slice_subtract_fusion = f32[31,128,1024]{2,1,0:T(8,128)S(1)} fusion(f32[31,128,1024]{2,1,0:T(8,128)} %bitcast.77, f32[32,128,1024]{2,1,0:T(8,128)} %param.3), kind=kLoop, calls=%fused_computation | loop fusion | flops 4063232 | bytes 48758784 | tf_op jit(solution)/shard_map/sub | solution.py:32
  283.8 12.0 %all-gather.35.cloned.1.call-done = bf16[1,1024,1024]{2,1,0:T(8,128)(2,1)} async-done(((bf16[1,128,1024]{2,1,0:T(8,128)(2,1)}), bf16[1,1024,1024]{2,1,0:T(8,128)(2,1)}) %all-gather.35.cloned.1.call-update) | async-done | bytes 2097168 | tf_op jit(solution)/shard_map/all_gather | solution.py:19
  298.6 139.8 %all-gather.23.cloned.1.call-done = bf16[3840,1024]{1,0:T(8,128)(2,1)} async-done(((bf16[3840,256]{1,0:T(8,128)(2,1)}), bf16[3840,1024]{1,0:T(8,128)(2,1)}) %all-gather.23.cloned.1.call-update) | async-done | bytes 7864336 | tf_op jit(solution)/shard_map/all_gather | solution.py:28
  438.3 28.4 %all-gather.21.cloned.1.call-done = bf16[1024,1024]{1,0:T(8,128)(2,1)} async-done(((bf16[128,1024]{1,0:T(8,128)(2,1)}), bf16[1024,1024]{1,0:T(8,128)(2,1)}) %all-gather.21.cloned.1.call-update) | async-done | bytes 2097168 | tf_op jit(solution)/shard_map/all_gather | solution.py:22
  466.8 15.3 %convolution_bitcast_fusion.2 = f32[3840,1024]{0,1:T(8,128)} fusion(bf16[1024,1024]{1,0:T(8,128)(2,1)} %all-gather.21.cloned.1.call-done, bf16[3840,1024]{1,0:T(8,128)(2,1)} %all-gather.23.cloned.1.call-done), kind=kOutput, calls=%fused_computation.6 | convolution fusion | flops 8053063680 | bytes 25690112 | tf_op jit(solution)/shard_map/dot_general | solution.py:27
  482.1 15.7 %copy.16 = f32[3840,1024]{1,0:T(8,128)} copy(f32[3840,1024]{0,1:T(8,128)} %convolution_bitcast_fusion.2) | data formatting | bytes 31457280 | tf_op jit(solution)/shard_map/dot_general | solution.py:27
  497.8 11.2 %slice_subtract_fusion.1 = f32[30,128,1024]{2,1,0:T(8,128)S(1)} fusion(f32[30,128,1024]{2,1,0:T(8,128)} %bitcast.78, f32[31,128,1024]{2,1,0:T(8,128)} %copy-done), kind=kLoop, calls=%fused_computation.1 | loop fusion | flops 3932160 | bytes 47185920 | tf_op jit(solution)/shard_map/sub | solution.py:32
  528.8 14.4 %all-gather.37.cloned.1.call-done = bf16[1,1024,1024]{2,1,0:T(8,128)(2,1)} async-done(((bf16[1,128,1024]{2,1,0:T(8,128)(2,1)}), bf16[1,1024,1024]{2,1,0:T(8,128)(2,1)}) %all-gather.37.cloned.1.call-update) | async-done | bytes 2097168 | tf_op jit(solution)/shard_map/all_gather | solution.py:19
  546.1 135.5 %all-gather.27.cloned.1.call-done = bf16[3712,1024]{1,0:T(8,128)(2,1)} async-done(((bf16[3712,256]{1,0:T(8,128)(2,1)}), bf16[3712,1024]{1,0:T(8,128)(2,1)}) %all-gather.27.cloned.1.call-update) | async-done | bytes 7602192 | tf_op jit(solution)/shard_map/all_gather | solution.py:28
  681.6 28.6 %all-gather.25.cloned.1.call-done = bf16[1024,1024]{1,0:T(8,128)(2,1)} async-done(((bf16[128,1024]{1,0:T(8,128)(2,1)}), bf16[1024,1024]{1,0:T(8,128)(2,1)}) %all-gather.25.cloned.1.call-update) | async-done | bytes 2097168 | tf_op jit(solution)/shard_map/all_gather | solution.py:22
  710.2 15.1 %convolution_bitcast_fusion.1 = f32[3712,1024]{0,1:T(8,128)} fusion(bf16[1024,1024]{1,0:T(8,128)(2,1)} %all-gather.25.cloned.1.call-done, bf16[3712,1024]{1,0:T(8,128)(2,1)} %all-gather.27.cloned.1.call-done), kind=kOutput, calls=%fused_computation.5 | convolution fusion | flops 7784628224 | bytes 24903680 | tf_op jit(solution)/shard_map/dot_general | solution.py:27
  725.3 15.5 %copy.19 = f32[3712,1024]{1,0:T(8,128)} copy(f32[3712,1024]{0,1:T(8,128)} %convolution_bitcast_fusion.1) | data formatting | bytes 30408704 | tf_op jit(solution)/shard_map/dot_general | solution.py:27
  740.8 10.8 %slice_subtract_fusion.2 = f32[29,128,1024]{2,1,0:T(8,128)S(1)} fusion(f32[29,128,1024]{2,1,0:T(8,128)} %bitcast.79, f32[30,128,1024]{2,1,0:T(8,128)} %copy-done.1), kind=kLoop, calls=%fused_computation.2 | loop fusion | flops 3801088 | bytes 45613056 | tf_op jit(solution)/shard_map/sub | solution.py:32
  767.3 18.5 %all-gather.39.cloned.1.call-done = bf16[1,1024,1024]{2,1,0:T(8,128)(2,1)} async-done(((bf16[1,128,1024]{2,1,0:T(8,128)(2,1)}), bf16[1,1024,1024]{2,1,0:T(8,128)(2,1)}) %all-gather.39.cloned.1.call-update) | async-done | bytes 2097168 | tf_op jit(solution)/shard_map/all_gather | solution.py:19
  791.3 128.7 %all-gather.31.cloned.1.call-done = bf16[3584,1024]{1,0:T(8,128)(2,1)} async-done(((bf16[3584,256]{1,0:T(8,128)(2,1)}), bf16[3584,1024]{1,0:T(8,128)(2,1)}) %all-gather.31.cloned.1.call-update) | async-done | bytes 7340048 | tf_op jit(solution)/shard_map/all_gather | solution.py:28
  920.0 27.9 %all-gather.29.cloned.1.call-done = bf16[1024,1024]{1,0:T(8,128)(2,1)} async-done(((bf16[128,1024]{1,0:T(8,128)(2,1)}), bf16[1024,1024]{1,0:T(8,128)(2,1)}) %all-gather.29.cloned.1.call-update) | async-done | bytes 2097168 | tf_op jit(solution)/shard_map/all_gather | solution.py:22
  947.8 13.8 %convolution_bitcast_fusion = f32[3584,1024]{0,1:T(8,128)} fusion(bf16[1024,1024]{1,0:T(8,128)(2,1)} %all-gather.29.cloned.1.call-done, bf16[3584,1024]{1,0:T(8,128)(2,1)} %all-gather.31.cloned.1.call-done), kind=kOutput, calls=%fused_computation.4 | convolution fusion | flops 7516192768 | bytes 24117248 | tf_op jit(solution)/shard_map/dot_general | solution.py:27
  961.6 15.4 %copy.22 = f32[3584,1024]{1,0:T(8,128)} copy(f32[3584,1024]{0,1:T(8,128)} %convolution_bitcast_fusion) | data formatting | bytes 29360128 | tf_op jit(solution)/shard_map/dot_general | solution.py:27
  977.1 15.2 %slice_subtract_fusion.3 = f32[28,128,1024]{2,1,0:T(8,128)} fusion(f32[28,128,1024]{2,1,0:T(8,128)} %bitcast.80, f32[29,128,1024]{2,1,0:T(8,128)} %copy-done.2), kind=kLoop, calls=%fused_computation.3 | loop fusion | flops 3670016 | bytes 44040192 | tf_op jit(solution)/shard_map/sub | solution.py:32
  (49 shorter events, 84.8 us)
Async XLA Ops:
  7.2 33.9 %all-gather.33.cloned.1.call-start = ((), (), s32[]{:S(2)}) async-start(), calls=%async_computation.8 | async-start | bytes 2359296 | tf_op jit(solution)/shard_map/all_gather | solution.py:19
  9.0 63.0 %all-gather.17.cloned.1.call-start = ((), (), s32[]{:S(2)}) async-start(), calls=%async_computation | async-start | bytes 2359296 | tf_op jit(solution)/shard_map/all_gather | solution.py:22
  44.0 175.1 %all-gather.19.cloned.1.call-start = ((), (), s32[]{:S(2)}) async-start(), calls=%async_computation.1 | async-start | bytes 10158080 | tf_op jit(solution)/shard_map/all_gather | solution.py:28
  56.8 239.0 %all-gather.35.cloned.1.call-start = ((), (), s32[]{:S(2)}) async-start(), calls=%async_computation.9 | async-start | bytes 2359296 | tf_op jit(solution)/shard_map/all_gather | solution.py:19
  263.2 5.6 copy-start
  269.5 26.2 %copy-start.3 = (bf16[4,128,1024]{2,1,0:T(8,128)(2,1)S(1)}, bf16[4,128,1024]{2,1,0:T(8,128)(2,1)}, u32[]{:S(2)}) copy-start(bf16[4,128,1024]{2,1,0:T(8,128)(2,1)} %param.5) | copy-start | bytes 3145732
  269.5 168.8 %all-gather.23.cloned.1.call-start = ((), (), s32[]{:S(2)}) async-start(), calls=%async_computation.3 | async-start | bytes 9830400 | tf_op jit(solution)/shard_map/all_gather | solution.py:28
  283.7 183.0 %all-gather.21.cloned.1.call-start = ((), (), s32[]{:S(2)}) async-start(), calls=%async_computation.2 | async-start | bytes 2359296 | tf_op jit(solution)/shard_map/all_gather | solution.py:22
  298.5 244.6 %all-gather.37.cloned.1.call-start = ((), (), s32[]{:S(2)}) async-start(), calls=%async_computation.10 | async-start | bytes 2359296 | tf_op jit(solution)/shard_map/all_gather | solution.py:19
  508.9 5.4 copy-start.1
  515.1 166.5 %all-gather.27.cloned.1.call-start = ((), (), s32[]{:S(2)}) async-start(), calls=%async_computation.5 | async-start | bytes 9502720 | tf_op jit(solution)/shard_map/all_gather | solution.py:28
  528.7 181.4 %all-gather.25.cloned.1.call-start = ((), (), s32[]{:S(2)}) async-start(), calls=%async_computation.4 | async-start | bytes 2359296 | tf_op jit(solution)/shard_map/all_gather | solution.py:22
  546.1 239.7 %all-gather.39.cloned.1.call-start = ((), (), s32[]{:S(2)}) async-start(), calls=%async_computation.11 | async-start | bytes 2359296 | tf_op jit(solution)/shard_map/all_gather | solution.py:19
  751.6 5.3 copy-start.2
  757.8 162.2 %all-gather.31.cloned.1.call-start = ((), (), s32[]{:S(2)}) async-start(), calls=%async_computation.7 | async-start | bytes 9175040 | tf_op jit(solution)/shard_map/all_gather | solution.py:28
  767.2 180.6 %all-gather.29.cloned.1.call-start = ((), (), s32[]{:S(2)}) async-start(), calls=%async_computation.6 | async-start | bytes 2359296 | tf_op jit(solution)/shard_map/all_gather | solution.py:22
Sparse Core Ops, SparseCore 0:
  10.5 30.5 all-gather.32
  44.1 27.8 all-gather.16
  74.1 144.8 all-gather.18
  269.6 26.0 all-gather.34
  297.7 140.5 all-gather.22
  440.6 26.0 all-gather.20
  515.2 27.8 all-gather.36
  545.3 136.2 all-gather.26
  684.1 26.0 all-gather.24
  757.9 27.8 all-gather.38
  787.9 131.9 all-gather.30
  921.7 26.0 all-gather.28
where the time goes:
time: 1010 us; the launch traced here: 1000 us
  waiting for transfers between devices  728 us (72%)
  local copies, waits for them, and re-layouts  133 us (13%)
  matrix products  71.6 us (7%)
  other arithmetic  51.3 us (5%)
  between operations  14.7 us (1%)
    all_gather x4, waiting for transfers between devices, shards(): lax.all_gather(flat_tiles, 'col', axis=1, tiled=True)  551 us
    all_gather x4, waiting for transfers between devices, shards(): lax.all_gather(own_rows.astype(jnp.bfloat16), 'row', axis=0, tiled=True)  100 us
    all_gather x4, waiting for transfers between devices, shards(): lax.all_gather(current, 'row', axis=0, tiled=True)  76.9 us
    dot_general x4, local copies, waits for them, and re-layouts, shards(): jnp.dot(lax.all_gather(flat_tiles, 'col', axis=1, tiled=True), whole_solv...  63.3 us
    dot_general x4, matrix products, shards(): jnp.dot(lax.all_gather(flat_tiles, 'col', axis=1, tiled=True), whole_solv...  60.2 us
    sub x4, other arithmetic, shards(): remaining_rows[1:] - update.reshape(later_count, tile_rows, rhs_width)  48.7 us
    slice x4, local copies, waits for them, and re-layouts, shards(): lower_tiles = factor[section + 1:, :, section, :]  35.9 us
    unnamed x12, local copies, waits for them, and re-layouts  29.6 us
  transfers between devices with their start and end apart: 12, of which 12 were waited for; matrix products, arithmetic and copies ran while one was open for 6% of the time, Pallas kernels for 0%

commit v1 on v0

v1 whole, which is shorter than its diff:
```python
import jax
import jax.numpy as jnp
from jax import lax
from jax.sharding import PartitionSpec as P

STEPS = 4
GATHERED = (7, 7, 7, 7)
REDUCED = ()


def dot(a, b):
    return jnp.dot(a, b, preferred_element_type=jnp.float32)


def up(n, distance):
    return [(z, z + 1) for z in range(distance - 1, n - 1)]


def down(n, distance):
    return [(z, z - 1) for z in range(1, n - distance + 1)]


class Line:
    def __init__(self, own, n):
        self.n = n
        self.own = own
        self.below = [own]
        self.above = [own]

    def hop(self):
        distance = len(self.below)
        self.below.append(lax.ppermute(self.below[-1], "col", up(self.n, distance)))
        self.above.append(lax.ppermute(self.above[-1], "col", down(self.n, distance)))

    def tie(self, value):
        value, self.below[-1], self.above[-1] = lax.optimization_barrier((value, self.below[-1], self.above[-1]))
        return value

    def parts(self):
        while len(self.below) < self.n:
            self.hop()
        z = lax.axis_index("col")
        return [self.own] + [
            jnp.where(z + d < self.n, self.above[d], self.below[self.n - d]) for d in range(1, self.n)
        ]


def reduce_line(products, n):
    upward = downward = None
    for distance in range(n - 1, 0, -1):
        u = products[distance]
        v = products[n - distance]
        if upward is not None:
            u = u + upward.astype(jnp.float32)
            v = v + downward.astype(jnp.float32)
        upward = lax.ppermute(u.astype(jnp.bfloat16), "col", [(z, z + 1) for z in range(n - distance)])
        downward = lax.ppermute(v.astype(jnp.bfloat16), "col", [(z, z - 1) for z in range(distance, n)])
    return products[0] + upward.astype(jnp.float32) + downward.astype(jnp.float32)


def shards(rhs, factor, diag_inverse):
    block_count, tile_rows, width = rhs.shape
    panel = factor.shape[3]
    n = lax.axis_size("col")
    rows_n = lax.axis_size("row")
    z = lax.axis_index("col")
    r = lax.axis_index("row")

    first = rhs[0].astype(jnp.bfloat16)
    whole = lax.all_gather(first, "row", axis=0, tiled=True)
    head = factor[1:STEPS, :, : STEPS - 1, :].reshape((STEPS - 1) * tile_rows, (STEPS - 1) * panel)
    head_parts = jnp.stack(Line(head, n).parts())
    head_parts = head_parts.reshape(n, STEPS - 1, tile_rows, STEPS - 1, panel)

    tiles = []
    start = STEPS
    for count in GATHERED:
        flat = factor[start : start + count].reshape(count * tile_rows, STEPS * panel)
        tiles.append((start, count, Line(flat, n)))
        start += count

    order = [line for _ in range(1, n) for _, _, line in tiles]

    def advance(value):
        if not order:
            return value
        line = order.pop(0)
        line.hop()
        return line.tie(value)

    solved = []
    solution_list = []
    for k in range(STEPS):
        if k:
            total = rhs[k]
            for d in range(n):
                part = lax.dynamic_slice_in_dim(jnp.stack(solved), ((z + d) % n) * panel, panel, axis=1)
                total = total - dot(head_parts[d, k - 1, :, :k, :].reshape(tile_rows, k * panel), part.reshape(k * panel, width))
            whole = lax.all_gather(total.astype(jnp.bfloat16), "row", axis=0, tiled=True)
        own = dot(diag_inverse[k], advance(whole))
        solution_list.append(own)
        solved.append(advance(lax.all_gather(own.astype(jnp.bfloat16), "row", axis=0, tiled=True)))
    stacked = jnp.stack(solved)

    def panel_of(d):
        return lax.dynamic_slice_in_dim(stacked, ((z + d) % n) * panel, panel, axis=1).reshape(STEPS * panel, width)

    panels = [panel_of(d) for d in range(n)]
    outs = []
    for begin, count, line in tiles:
        parts = line.parts()
        total = rhs[begin : begin + count].reshape(count * tile_rows, width)
        for d in range(n):
            total = total - dot(parts[d], panels[d])
        outs.append(total.reshape(count, tile_rows, width))

    if REDUCED:
        share = panel // rows_n
        pieces = []
        for d in range(1, n):
            target = (z - d) % n
            piece = lax.dynamic_slice_in_dim(stacked, target * panel + r * share, share, axis=1)
            pieces.append(lax.ppermute(piece, "col", [(s, (s - d) % n) for s in range(n)]))
        spread = lax.all_gather(jnp.concatenate(pieces, axis=2), "row", axis=1, tiled=True)
        spread = spread.reshape(STEPS * panel, (n - 1) * width)
        own_panels = [panels[0]] + [spread[:, d * width : (d + 1) * width] for d in range(n - 1)]
        for count in REDUCED:
            flat = factor[start : start + count].reshape(count * tile_rows, STEPS * panel)
            total = reduce_line([dot(flat, p) for p in own_panels], n)
            outs.append(rhs[start : start + count] - total.reshape(count, tile_rows, width))
            start += count
    return jnp.stack(solution_list), jnp.concatenate(outs)


def solution(mesh):
    in_specs = (P(None, "row", "col"), P(None, "row", None, "col"), P(None, "row", None))
    out_specs = (P(None, "row", "col"), P(None, "row", "col"))
    return jax.shard_map(shards, mesh=mesh, in_specs=in_specs, out_specs=out_specs, check_vma=False)
```

time: 1010 us -> 648 us (0.64)
  waiting for transfers between devices: 728 us -> 338 us
  starting transfers between devices: 1.14 us -> 69.6 us
  local copies, waits for them, and re-layouts: 133 us -> 94.2 us
  other arithmetic: 51.3 us -> 21.1 us
  matrix products: 71.6 us -> 101 us
    all_gather x12 -> x8, waiting for transfers between devices: 728 us -> 0.03 us  [the longest x4 0.03 us: shards(): lax.all_gather(own.astype(jnp.bfloat16), 'row', axis=0, tiled=True)]
    ppermute x0 -> x30, waiting for transfers between devices: none -> 337 us  [the longest x15 235 us: hop(): lax.ppermute(self.above[-1], 'col', down(self.n, distance))]
    ppermute x0 -> x30, starting transfers between devices: none -> 69.3 us  [the longest x15 38.7 us: hop(): self.below.append(lax.ppermute(self.below[-1], 'col', up(self.n, distance)))]
    dot_general x4 -> x0, local copies, waits for them, and re-layouts: 63.3 us -> none  [shards(): jnp.dot(lax.all_gather(flat_tiles, 'col', axis=1, tiled=True), whole_solv...]
    sub x4 -> x0, other arithmetic: 48.7 us -> none  [shards(): remaining_rows[1:] - update.reshape(later_count, tile_rows, rhs_width)]
    dynamic_slice x0 -> x14, local copies, waits for them, and re-layouts: none -> 38.2 us  [the longest x9 21.7 us: shards(): lax.dynamic_slice_in_dim(jnp.stack(solved), (z + d) % n * panel, panel, a...]
    dot_general x8 -> x32, matrix products: 71.6 us -> 101 us  [dot(): return jnp.dot(a, b, preferred_element_type=jnp.float32)]
    unnamed x12 -> x89, local copies, waits for them, and re-layouts: 29.6 us -> 17.5 us
  transfers between devices with their start and end apart: 12 -> 38, of which waited for: 12 -> 17; matrix products, arithmetic and copies ran while one was open for 6% -> 23% of each run, Pallas kernels for 0% -> 0%
where the time goes in v1:
time: 648 us; the launch traced here: 639 us
  waiting for transfers between devices  338 us (52%)
  matrix products  101 us (16%)
  local copies, waits for them, and re-layouts  94.2 us (15%)
  starting transfers between devices  69.6 us (11%)
  other arithmetic  21.1 us (3%)
  between operations  15.4 us (2%)
    ppermute x15, waiting for transfers between devices, hop(): lax.ppermute(self.above[-1], 'col', down(self.n, distance))  235 us
    ppermute x15, waiting for transfers between devices, hop(): self.below.append(lax.ppermute(self.below[-1], 'col', up(self.n, distance)))  103 us
    dot_general x32, matrix products, dot(): return jnp.dot(a, b, preferred_element_type=jnp.float32)  101 us
    ppermute x15, starting transfers between devices, hop(): self.below.append(lax.ppermute(self.below[-1], 'col', up(self.n, distance)))  38.7 us
    ppermute x15, starting transfers between devices, hop(): lax.ppermute(self.above[-1], 'col', down(self.n, distance))  30.6 us
    dynamic_slice x9, local copies, waits for them, and re-layouts, shards(): lax.dynamic_slice_in_dim(jnp.stack(solved), (z + d) % n * panel, panel, a...  21.7 us
    unnamed x89, local copies, waits for them, and re-layouts  17.5 us
    dynamic_slice x5, local copies, waits for them, and re-layouts, panel_of(): lax.dynamic_slice_in_dim(stacked, (z + d) % n * panel, panel, axis=1)  16.5 us
  transfers between devices with their start and end apart: 38, of which 17 were waited for; matrix products, arithmetic and copies ran while one was open for 23% of the time, Pallas kernels for 0%

profile of v1, /device:TPU:0, one launch (start us, length us, event | category | flops | bytes accessed | tf_op | source)
XLA Modules:
  0.0 639.4 jit_solution(1843927264934609274)
XLA Ops:
  9.1 7.1 %fusion.100 = (bf16[7,128,4,256]{3,2,1,0:T(4,128)(2,1)}, bf16[7,128,4,256]{3,2,1,0:T(4,128)(2,1)S(1)}, bf16[7,128,4,256]{3,2,1,0:T(4,128)(2,1)S(1)}, bf16[7,128,4,256]{3,2,1,0:T(4,128)(2,1)}) fusion(bf16[32,128,4,256]{3,2,1,0:T(4,128)(2,1)} %param.4), kind=kLoop, calls=%fused_computation.135 | loop fusion | bytes 14680064 | tf_op jit(solution)/shard_map/slice | solution.py:78
  22.9 37.8 %collective-permute-done = bf16[896,1024]{1,0:T(8,128)(2,1)S(1)} collective-permute-done((bf16[896,1024]{1,0:T(8,128)(2,1)S(1)}, bf16[896,1024]{1,0:T(8,128)(2,1)S(1)}, u32[]{:S(2)}, u32[]{:S(2)}) %collective-permute-start) | collective-permute-done | bytes 1835040 | tf_op jit(solution)/shard_map/ppermute | solution.py:32
  76.3 5.8 collective-permute-start.2
  94.3 46.6 %collective-permute-done.8 = bf16[384,768]{1,0:T(8,128)(2,1)} collective-permute-done((bf16[384,768]{1,0:T(8,128)(2,1)S(1)}, bf16[384,768]{1,0:T(8,128)(2,1)}, u32[]{:S(2)}, u32[]{:S(2)}) %collective-permute-start.8) | collective-permute-done | bytes 589856 | tf_op jit(solution)/shard_map/ppermute | solution.py:33
  148.7 7.1 %collective-permute-done.9 = bf16[384,768]{1,0:T(8,128)(2,1)} collective-permute-done((bf16[384,768]{1,0:T(8,128)(2,1)}, bf16[384,768]{1,0:T(8,128)(2,1)}, u32[]{:S(2)}, u32[]{:S(2)}) %collective-permute-start.9) | collective-permute-done | bytes 589856 | tf_op jit(solution)/shard_map/ppermute | solution.py:33
  169.5 34.8 %collective-permute-done.10 = bf16[896,1024]{1,0:T(8,128)(2,1)S(1)} collective-permute-done((bf16[896,1024]{1,0:T(8,128)(2,1)S(1)}, bf16[896,1024]{1,0:T(8,128)(2,1)S(1)}, u32[]{:S(2)}, u32[]{:S(2)}) %collective-permute-start.10) | collective-permute-done | bytes 1835040 | tf_op jit(solution)/shard_map/ppermute | solution.py:32
  227.4 26.6 %collective-permute-done.12 = bf16[896,1024]{1,0:T(8,128)(2,1)} collective-permute-done((bf16[896,1024]{1,0:T(8,128)(2,1)}, bf16[896,1024]{1,0:T(8,128)(2,1)}, u32[]{:S(2)}, u32[]{:S(2)}) %collective-permute-start.12) | collective-permute-done | bytes 1835040 | tf_op jit(solution)/shard_map/ppermute | solution.py:32
  254.0 5.4 collective-permute-done.13
  278.8 37.8 %collective-permute-done.15 = bf16[896,1024]{1,0:T(8,128)(2,1)} collective-permute-done((bf16[896,1024]{1,0:T(8,128)(2,1)}, bf16[896,1024]{1,0:T(8,128)(2,1)}, u32[]{:S(2)}, u32[]{:S(2)}) %collective-permute-start.15) | collective-permute-done | bytes 1835040 | tf_op jit(solution)/shard_map/ppermute | solution.py:33
  328.1 31.9 %collective-permute-done.17 = bf16[896,1024]{1,0:T(8,128)(2,1)} collective-permute-done((bf16[896,1024]{1,0:T(8,128)(2,1)}, bf16[896,1024]{1,0:T(8,128)(2,1)}, u32[]{:S(2)}, u32[]{:S(2)}) %collective-permute-start.17) | collective-permute-done | bytes 1835040 | tf_op jit(solution)/shard_map/ppermute | solution.py:33
  386.0 36.1 %collective-permute-done.19 = bf16[896,1024]{1,0:T(8,128)(2,1)} collective-permute-done((bf16[896,1024]{1,0:T(8,128)(2,1)}, bf16[896,1024]{1,0:T(8,128)(2,1)}, u32[]{:S(2)}, u32[]{:S(2)}) %collective-permute-start.19) | collective-permute-done | bytes 1835040 | tf_op jit(solution)/shard_map/ppermute | solution.py:33
  427.4 12.0 %collective-permute-start.21 = (bf16[896,1024]{1,0:T(8,128)(2,1)}, bf16[896,1024]{1,0:T(8,128)(2,1)}, u32[]{:S(2)}, u32[]{:S(2)}) collective-permute-start(bf16[896,1024]{1,0:T(8,128)(2,1)} %collective-permute-done.13), channel_id=1, source_target_pairs={{1,0},{2,1},{5,4},{6,5},{9,8},{10,9},{13,12},{14,13},{17,16},{18,1... | collective-permute-start | bytes 5505032 | tf_op jit(solution)/shard_map/ppermute | solution.py:33
  439.4 12.7 %fusion.98 = (f32[7,128,1024]{2,1,0:T(8,128)}, f32[7,128,1024]{2,1,0:T(8,128)}, f32[7,128,1024]{2,1,0:T(8,128)}, f32[7,128,1024]{2,1,0:T(8,128)}) fusion(f32[32,128,1024]{2,1,0:T(8,128)} %param.3), kind=kLoop, calls=%fused_computation.133 | loop fusion | bytes 29360128 | tf_op jit(solution)/shard_map/slice | solution.py:112
  464.0 9.1 %collective-permute-done.21 = bf16[896,1024]{1,0:T(8,128)(2,1)} collective-permute-done((bf16[896,1024]{1,0:T(8,128)(2,1)}, bf16[896,1024]{1,0:T(8,128)(2,1)}, u32[]{:S(2)}, u32[]{:S(2)}) %collective-permute-start.21) | collective-permute-done | bytes 1835040 | tf_op jit(solution)/shard_map/ppermute | solution.py:33
  485.9 6.2 fusion.32
  492.1 5.4 fusion.26
  497.5 5.4 fusion.20
  535.4 16.3 %collective-permute-done.25 = bf16[896,1024]{1,0:T(8,128)(2,1)} collective-permute-done((bf16[896,1024]{1,0:T(8,128)(2,1)}, bf16[896,1024]{1,0:T(8,128)(2,1)}, u32[]{:S(2)}, u32[]{:S(2)}) %collective-permute-start.25) | collective-permute-done | bytes 1835040 | tf_op jit(solution)/shard_map/ppermute | solution.py:33
  560.1 5.6 fusion.22
  573.3 17.7 %collective-permute-done.27 = bf16[896,1024]{1,0:T(8,128)(2,1)} collective-permute-done((bf16[896,1024]{1,0:T(8,128)(2,1)}, bf16[896,1024]{1,0:T(8,128)(2,1)}, u32[]{:S(2)}, u32[]{:S(2)}) %collective-permute-start.27) | collective-permute-done | bytes 1835040 | tf_op jit(solution)/shard_map/ppermute | solution.py:33
  591.0 6.3 fusion.5
  597.4 6.2 fusion.16
  603.6 17.4 %collective-permute-done.29 = bf16[896,1024]{1,0:T(8,128)(2,1)} collective-permute-done((bf16[896,1024]{1,0:T(8,128)(2,1)}, bf16[896,1024]{1,0:T(8,128)(2,1)}, u32[]{:S(2)}, u32[]{:S(2)}) %collective-permute-start.29) | collective-permute-done | bytes 1835040 | tf_op jit(solution)/shard_map/ppermute | solution.py:33
  626.3 5.8 pad_maximum_fusion
  (230 shorter events, 220.9 us)
Async XLA Ops:
  7.2 58.0 %all-gather.24.cloned.1.call-start = ((), (), s32[]{:S(2)}) async-start(), calls=%async_computation.7 | async-start | bytes 2359296 | tf_op jit(solution)/shard_map/all_gather | solution.py:70
  9.0 150.6 %all-gather.10.cloned.1.call-start = ((), (), s32[]{:S(2)}) async-start(), calls=%async_computation | async-start | bytes 2359296 | tf_op jit(solution)/shard_map/all_gather | solution.py:102
  16.6 44.2 %collective-permute-start = (bf16[896,1024]{1,0:T(8,128)(2,1)S(1)}, bf16[896,1024]{1,0:T(8,128)(2,1)S(1)}, u32[]{:S(2)}, u32[]{:S(2)}) collective-permute-start(bf16[896,1024]{1,0:T(8,128)(2,1)S(1)} %bitcast.254), channel_id=1, source_target_pairs={{0,1},{1,2},{2,3},{4,5},{5,6},{6,7},{8,9},{9,10},{10,11},{12,13},{... | collective-permute-start | bytes 5505032 | tf_op jit(solution)/shard_map/ppermute | solution.py:32
  21.6 43.5 %collective-permute-start.1 = (bf16[896,1024]{1,0:T(8,128)(2,1)S(1)}, bf16[896,1024]{1,0:T(8,128)(2,1)}, u32[]{:S(2)}, u32[]{:S(2)}) collective-permute-start(bf16[896,1024]{1,0:T(8,128)(2,1)S(1)} %bitcast.255), channel_id=1, source_target_pairs={{1,0},{2,1},{3,2},{5,4},{6,5},{7,6},{9,8},{10,9},{11,10},{13,12},{... | collective-permute-start | bytes 5505032 | tf_op jit(solution)/shard_map/ppermute | solution.py:33
  68.3 140.3 %all-gather.12.cloned.1.call-start = ((), (), s32[]{:S(2)}) async-start(), calls=%async_computation.1 | async-start | bytes 2359296 | tf_op jit(solution)/shard_map/all_gather | solution.py:99
  76.3 83.4 %collective-permute-start.2 = (bf16[896,1024]{1,0:T(8,128)(2,1)}, bf16[896,1024]{1,0:T(8,128)(2,1)}, u32[]{:S(2)}, u32[]{:S(2)}) collective-permute-start(bf16[896,1024]{1,0:T(8,128)(2,1)} %bitcast.66), channel_id=1, source_target_pairs={{0,1},{1,2},{2,3},{4,5},{5,6},{6,7},{8,9},{9,10},{10,11},{12,13},{... | collective-permute-start | bytes 5505032 | tf_op jit(solution)/shard_map/ppermute | solution.py:32
  82.1 77.6 %collective-permute-start.3 = (bf16[896,1024]{1,0:T(8,128)(2,1)}, bf16[896,1024]{1,0:T(8,128)(2,1)}, u32[]{:S(2)}, u32[]{:S(2)}) collective-permute-start(bf16[896,1024]{1,0:T(8,128)(2,1)} %bitcast.66), channel_id=1, source_target_pairs={{1,0},{2,1},{3,2},{5,4},{6,5},{7,6},{9,8},{10,9},{11,10},{13,12},{... | collective-permute-start | bytes 5505032 | tf_op jit(solution)/shard_map/ppermute | solution.py:33
  91.5 49.4 %collective-permute-start.8 = (bf16[384,768]{1,0:T(8,128)(2,1)S(1)}, bf16[384,768]{1,0:T(8,128)(2,1)}, u32[]{:S(2)}, u32[]{:S(2)}) collective-permute-start(bf16[384,768]{1,0:T(8,128)(2,1)S(1)} %collective-permute-done.4), channel_id=1, source_target_pairs={{1,0},{2,1},{5,4},{6,5},{9,8},{10,9},{13,12},{14,13},{17,16},{18,1... | collective-permute-start | bytes 1769480 | tf_op jit(solution)/shard_map/ppermute | solution.py:33
  92.8 54.6 %collective-permute-start.7 = (bf16[384,768]{1,0:T(8,128)(2,1)}, bf16[384,768]{1,0:T(8,128)(2,1)}, u32[]{:S(2)}, u32[]{:S(2)}) collective-permute-start(bf16[384,768]{1,0:T(8,128)(2,1)} %collective-permute-done.6), channel_id=1, source_target_pairs={{2,3},{6,7},{10,11},{14,15},{18,19},{22,23},{26,27},{30,31}} | collective-permute-start | bytes 1769480 | tf_op jit(solution)/shard_map/ppermute | solution.py:32
  164.8 94.6 %all-gather.14.cloned.1.call-start = ((), (), s32[]{:S(2)}) async-start(), calls=%async_computation.2 | async-start | bytes 2359296 | tf_op jit(solution)/shard_map/all_gather | solution.py:102
  168.2 40.4 %collective-permute-start.11 = (bf16[896,1024]{1,0:T(8,128)(2,1)S(1)}, bf16[896,1024]{1,0:T(8,128)(2,1)}, u32[]{:S(2)}, u32[]{:S(2)}) collective-permute-start(bf16[896,1024]{1,0:T(8,128)(2,1)S(1)} %bitcast.258), channel_id=1, source_target_pairs={{1,0},{2,1},{3,2},{5,4},{6,5},{7,6},{9,8},{10,9},{11,10},{13,12},{... | collective-permute-start | bytes 5505032 | tf_op jit(solution)/shard_map/ppermute | solution.py:33
  211.9 104.7 %all-gather.16.cloned.1.call-start = ((), (), s32[]{:S(2)}) async-start(), calls=%async_computation.3 | async-start | bytes 2359296 | tf_op jit(solution)/shard_map/all_gather | solution.py:99
  275.3 84.7 %all-gather.18.cloned.1.call-start = ((), (), s32[]{:S(2)}) async-start(), calls=%async_computation.4 | async-start | bytes 2359296 | tf_op jit(solution)/shard_map/all_gather | solution.py:102
  319.7 102.3 %all-gather.20.cloned.1.call-start = ((), (), s32[]{:S(2)}) async-start(), calls=%async_computation.5 | async-start | bytes 2359296 | tf_op jit(solution)/shard_map/all_gather | solution.py:99
  382.7 92.3 %all-gather.22.cloned.1.call-start = ((), (), s32[]{:S(2)}) async-start(), calls=%async_computation.6 | async-start | bytes 2359296 | tf_op jit(solution)/shard_map/all_gather | solution.py:102
  427.4 45.7 %collective-permute-start.21 = (bf16[896,1024]{1,0:T(8,128)(2,1)}, bf16[896,1024]{1,0:T(8,128)(2,1)}, u32[]{:S(2)}, u32[]{:S(2)}) collective-permute-start(bf16[896,1024]{1,0:T(8,128)(2,1)} %collective-permute-done.13), channel_id=1, source_target_pairs={{1,0},{2,1},{5,4},{6,5},{9,8},{10,9},{13,12},{14,13},{17,16},{18,1... | collective-permute-start | bytes 5505032 | tf_op jit(solution)/shard_map/ppermute | solution.py:33
  452.0 60.3 %collective-permute-start.22 = (bf16[896,1024]{1,0:T(8,128)(2,1)}, bf16[896,1024]{1,0:T(8,128)(2,1)}, u32[]{:S(2)}, u32[]{:S(2)}) collective-permute-start(bf16[896,1024]{1,0:T(8,128)(2,1)} %collective-permute-done.14), channel_id=1, source_target_pairs={{2,3},{6,7},{10,11},{14,15},{18,19},{22,23},{26,27},{30,31}} | collective-permute-start | bytes 5505032 | tf_op jit(solution)/shard_map/ppermute | solution.py:32
  453.9 71.9 %collective-permute-start.23 = (bf16[896,1024]{1,0:T(8,128)(2,1)}, bf16[896,1024]{1,0:T(8,128)(2,1)}, u32[]{:S(2)}, u32[]{:S(2)}) collective-permute-start(bf16[896,1024]{1,0:T(8,128)(2,1)} %collective-permute-done.15), channel_id=1, source_target_pairs={{1,0},{5,4},{9,8},{13,12},{17,16},{21,20},{25,24},{29,28}} | collective-permute-start | bytes 5505032 | tf_op jit(solution)/shard_map/ppermute | solution.py:33
  455.2 62.8 %collective-permute-start.24 = (bf16[896,1024]{1,0:T(8,128)(2,1)}, bf16[896,1024]{1,0:T(8,128)(2,1)}, u32[]{:S(2)}, u32[]{:S(2)}) collective-permute-start(bf16[896,1024]{1,0:T(8,128)(2,1)} %collective-permute-done.16), channel_id=1, source_target_pairs={{2,3},{6,7},{10,11},{14,15},{18,19},{22,23},{26,27},{30,31}} | collective-permute-start | bytes 5505032 | tf_op jit(solution)/shard_map/ppermute | solution.py:32
  462.7 89.0 %collective-permute-start.25 = (bf16[896,1024]{1,0:T(8,128)(2,1)}, bf16[896,1024]{1,0:T(8,128)(2,1)}, u32[]{:S(2)}, u32[]{:S(2)}) collective-permute-start(bf16[896,1024]{1,0:T(8,128)(2,1)} %collective-permute-done.17), channel_id=1, source_target_pairs={{1,0},{5,4},{9,8},{13,12},{17,16},{21,20},{25,24},{29,28}} | collective-permute-start | bytes 5505032 | tf_op jit(solution)/shard_map/ppermute | solution.py:33
  473.1 87.1 %collective-permute-start.26 = (bf16[896,1024]{1,0:T(8,128)(2,1)}, bf16[896,1024]{1,0:T(8,128)(2,1)}, u32[]{:S(2)}, u32[]{:S(2)}) collective-permute-start(bf16[896,1024]{1,0:T(8,128)(2,1)} %collective-permute-done.18), channel_id=1, source_target_pairs={{2,3},{6,7},{10,11},{14,15},{18,19},{22,23},{26,27},{30,31}} | collective-permute-start | bytes 5505032 | tf_op jit(solution)/shard_map/ppermute | solution.py:32
  512.3 78.7 %collective-permute-start.27 = (bf16[896,1024]{1,0:T(8,128)(2,1)}, bf16[896,1024]{1,0:T(8,128)(2,1)}, u32[]{:S(2)}, u32[]{:S(2)}) collective-permute-start(bf16[896,1024]{1,0:T(8,128)(2,1)} %collective-permute-done.19), channel_id=1, source_target_pairs={{1,0},{5,4},{9,8},{13,12},{17,16},{21,20},{25,24},{29,28}} | collective-permute-start | bytes 5505032 | tf_op jit(solution)/shard_map/ppermute | solution.py:33
  518.0 79.3 %collective-permute-start.28 = (bf16[896,1024]{1,0:T(8,128)(2,1)}, bf16[896,1024]{1,0:T(8,128)(2,1)}, u32[]{:S(2)}, u32[]{:S(2)}) collective-permute-start(bf16[896,1024]{1,0:T(8,128)(2,1)} %collective-permute-done.20), channel_id=1, source_target_pairs={{2,3},{6,7},{10,11},{14,15},{18,19},{22,23},{26,27},{30,31}} | collective-permute-start | bytes 5505032 | tf_op jit(solution)/shard_map/ppermute | solution.py:32
  525.8 95.2 %collective-permute-start.29 = (bf16[896,1024]{1,0:T(8,128)(2,1)}, bf16[896,1024]{1,0:T(8,128)(2,1)}, u32[]{:S(2)}, u32[]{:S(2)}) collective-permute-start(bf16[896,1024]{1,0:T(8,128)(2,1)} %collective-permute-done.21), channel_id=1, source_target_pairs={{1,0},{5,4},{9,8},{13,12},{17,16},{21,20},{25,24},{29,28}} | collective-permute-start | bytes 5505032 | tf_op jit(solution)/shard_map/ppermute | solution.py:33
  (55 other events, 873.5 us)
Sparse Core Ops, SparseCore 0:
  9.9 30.5 all-gather.23
  68.5 28.3 all-gather.9
  164.9 26.7 all-gather.11
  212.0 28.0 all-gather.13
  275.5 26.4 all-gather.15
  319.9 27.3 all-gather.17
  382.8 27.5 all-gather.19
  425.4 27.5 all-gather.21

commit v2 on v1

v2 whole, which is shorter than its diff:
```python
import functools

import jax
import jax.numpy as jnp
from jax import lax
from jax.experimental import pallas as pl
from jax.experimental.pallas import tpu as pltpu
from jax.sharding import PartitionSpec as P

STEPS = 4
GATHERED = (9, 9)
REDUCED = (5, 5)


def dot(a, b):
    return jnp.dot(a, b, preferred_element_type=jnp.float32)


def up(n, distance):
    return [(z, z + 1) for z in range(distance - 1, n - 1)]


def down(n, distance):
    return [(z, z - 1) for z in range(1, n - distance + 1)]


class Line:
    def __init__(self, own, n):
        self.n = n
        self.own = own
        self.below = [own]
        self.above = [own]

    def hop(self):
        distance = len(self.below)
        self.below.append(lax.ppermute(self.below[-1], "col", up(self.n, distance)))
        self.above.append(lax.ppermute(self.above[-1], "col", down(self.n, distance)))

    def tie(self, value):
        value, self.below[-1], self.above[-1] = lax.optimization_barrier((value, self.below[-1], self.above[-1]))
        return value

    def parts(self):
        while len(self.below) < self.n:
            self.hop()
        z = lax.axis_index("col")
        return [self.own] + [
            jnp.where(z + d < self.n, self.above[d], self.below[self.n - d]) for d in range(1, self.n)
        ]


class Sums:
    def __init__(self, products, n):
        self.n = n
        self.products = products
        self.distance = n
        self.upward = self.downward = None

    def hop(self):
        self.distance -= 1
        u = self.products[self.distance]
        v = self.products[self.n - self.distance]
        if self.upward is not None:
            u = u + self.upward.astype(jnp.float32)
            v = v + self.downward.astype(jnp.float32)
        self.upward = lax.ppermute(u.astype(jnp.bfloat16), "col", [(z, z + 1) for z in range(self.n - self.distance)])
        self.downward = lax.ppermute(v.astype(jnp.bfloat16), "col", [(z, z - 1) for z in range(self.distance, self.n)])

    def total(self):
        return self.products[0] + self.upward.astype(jnp.float32) + self.downward.astype(jnp.float32)


def substitute_kernel(rows_n, rhs_ref, head_ref, inverse_ref, solution_ref, solved_ref, current, solved, send_sem, recv_sem, out_sem):
    r = lax.axis_index("row")
    pair = r + 1 - 2 * (r % 2)
    half = rows_n // 2
    tile_rows, width = rhs_ref.shape[1:]
    columns = 256
    own_rows = pl.ds(pl.multiple_of(r * tile_rows, tile_rows), tile_rows)

    barrier = pltpu.get_barrier_semaphore()
    for j in range(1, rows_n):
        pl.semaphore_signal(barrier, inc=1, device_id={"row": (r + j) % rows_n}, device_id_type=pl.DeviceIdType.MESH)
    pl.semaphore_wait(barrier, rows_n - 1)

    sent = []

    def copy(buffer, exchange, owner, slot, device):
        rows = buffer.at[pl.ds(pl.multiple_of(owner * tile_rows, tile_rows), tile_rows)]
        return pltpu.make_async_remote_copy(
            src_ref=rows,
            dst_ref=rows,
            send_sem=send_sem.at[exchange, slot],
            recv_sem=recv_sem.at[exchange, owner],
            device_id={"row": device},
            device_id_type=pl.DeviceIdType.MESH,
        )

    def gather(buffer, exchange):
        for j in range(half - 1, 0, -1):
            sent.append(copy(buffer, exchange, r, j, (r + 2 * j) % rows_n))
            sent[-1].start()
        sent.append(copy(buffer, exchange, r, 0, pair))
        sent[-1].start()
        for j in range(1, half):
            owner = (r + rows_n - 2 * j) % rows_n
            onward = copy(buffer, exchange, owner, half + j, pair)
            onward.wait_recv()
            onward.start()
            sent.append(onward)
        for j in range(half):
            copy(buffer, exchange, (pair + rows_n - 2 * j) % rows_n, 0, pair).wait_recv()

    outward = []
    for k in range(rhs_ref.shape[0]):

        @pl.loop(0, width // columns)
        def _(c):
            cols = pl.ds(pl.multiple_of(c * columns, columns), columns)
            total = rhs_ref[k, :, cols]
            for j in range(k):
                total = total - dot(head_ref[k - 1, j], solved[j, :, cols])
            current[k, own_rows, cols] = total.astype(jnp.bfloat16)

        gather(current.at[k], 2 * k)

        @pl.loop(0, width // columns)
        def _(c):
            cols = pl.ds(pl.multiple_of(c * columns, columns), columns)
            own = dot(inverse_ref[k], current[k, :, cols])
            solution_ref[k, :, cols] = own
            solved[k, own_rows, cols] = own.astype(jnp.bfloat16)

        gather(solved.at[k], 2 * k + 1)
        outward.append(pltpu.make_async_copy(solved.at[k], solved_ref.at[k], out_sem.at[k]))
        outward[-1].start()
    for item in sent:
        item.wait_send()
    for item in outward:
        item.wait()


def substitute(rhs, head, inverse, rows_n):
    steps, tile_rows, width = rhs.shape
    block = rows_n * tile_rows
    vmem = pl.BlockSpec(memory_space=pltpu.VMEM)
    return pl.pallas_call(
        functools.partial(substitute_kernel, rows_n),
        out_shape=(
            jax.ShapeDtypeStruct((steps, tile_rows, width), jnp.float32),
            jax.ShapeDtypeStruct((steps, block, width), jnp.bfloat16),
        ),
        in_specs=[vmem] * 3,
        out_specs=(vmem, pl.BlockSpec(memory_space=pl.ANY)),
        scratch_shapes=[
            pltpu.VMEM((steps, block, width), jnp.bfloat16),
            pltpu.VMEM((steps, block, width), jnp.bfloat16),
            pltpu.SemaphoreType.DMA((2 * steps, rows_n)),
            pltpu.SemaphoreType.DMA((2 * steps, rows_n)),
            pltpu.SemaphoreType.DMA((steps,)),
        ],
        compiler_params=pltpu.CompilerParams(collective_id=0, has_side_effects=True, vmem_limit_bytes=40 * 2**20),
        cost_estimate=pl.CostEstimate(flops=12 * 10**13, bytes_accessed=2**24, transcendentals=0),
    )(rhs, head, inverse)


def shards(rhs, factor, diag_inverse):
    block_count, tile_rows, width = rhs.shape
    panel = factor.shape[3]
    n = lax.axis_size("col")
    rows_n = lax.axis_size("row")
    z = lax.axis_index("col")
    r = lax.axis_index("row")

    head = factor[1:STEPS, :, : STEPS - 1, :].transpose(0, 2, 1, 3)
    head = lax.all_gather(head, "col", axis=3, tiled=True)

    tiles = []
    start = STEPS
    for count in GATHERED:
        flat = factor[start : start + count].reshape(count * tile_rows, STEPS * panel)
        head, flat = lax.optimization_barrier((head, flat))
        tiles.append((start, count, Line(flat, n)))
        start += count

    solution_rows, stacked = substitute(rhs[:STEPS], head, diag_inverse, rows_n)
    for _, _, line in tiles:
        line.hop()
        stacked = line.tie(stacked)

    def panel_of(d):
        return lax.dynamic_slice_in_dim(stacked, ((z + d) % n) * panel, panel, axis=1).reshape(STEPS * panel, width)

    panels = [panel_of(d) for d in range(n)]
    share = panel // rows_n
    pieces = []
    for d in range(1, n):
        target = (z - d) % n
        piece = lax.dynamic_slice_in_dim(stacked, target * panel + r * share, share, axis=1)
        pieces.append(lax.ppermute(piece, "col", [(s, (s - d) % n) for s in range(n)]))
    spread = lax.all_gather(jnp.concatenate(pieces, axis=2), "row", axis=1, tiled=True)
    spread = spread.reshape(STEPS * panel, (n - 1) * width)
    own_panels = [panels[0]] + [spread[:, d * width : (d + 1) * width] for d in range(n - 1)]
    sums = []
    for count in REDUCED:
        flat = factor[start : start + count].reshape(count * tile_rows, STEPS * panel)
        sums.append((start, count, Sums([dot(flat, p) for p in own_panels], n)))
        start += count

    for step in range(1, n):
        if step < n - 1:
            for _, _, line in tiles:
                line.hop()
        for _, _, item in sums:
            item.hop()
        moved = [(line.below[-1], line.above[-1]) for _, _, line in tiles]
        carried = [(item.upward, item.downward) for _, _, item in sums]
        if step < n - 1:
            moved, carried = lax.optimization_barrier((moved, carried))
        for (_, _, line), (below, above) in zip(tiles, moved):
            line.below[-1], line.above[-1] = below, above
        for (_, _, item), (upward, downward) in zip(sums, carried):
            item.upward, item.downward = upward, downward

    outs = []
    for begin, count, line in tiles:
        parts = line.parts()
        total = rhs[begin : begin + count].reshape(count * tile_rows, width)
        for d in range(n):
            total = total - dot(parts[d], panels[d])
        outs.append(total.reshape(count, tile_rows, width))
    for begin, count, item in sums:
        outs.append(rhs[begin : begin + count] - item.total().reshape(count, tile_rows, width))
    return solution_rows, jnp.concatenate(outs)


def solution(mesh):
    in_specs = (P(None, "row", "col"), P(None, "row", None, "col"), P(None, "row", None))
    out_specs = (P(None, "row", "col"), P(None, "row", "col"))
    return jax.shard_map(shards, mesh=mesh, in_specs=in_specs, out_specs=out_specs, check_vma=False)
```

time: 648 us -> 627 us (0.968)
  Pallas kernels: 0 us -> 138 us
  waiting for transfers between devices: 338 us -> 231 us
  local copies, waits for them, and re-layouts: 94.2 us -> 43.5 us
  matrix products: 101 us -> 81.2 us
  starting transfers between devices: 69.6 us -> 83 us
  other arithmetic: 21.1 us -> 27.7 us
    ppermute x15 -> x6, waiting for transfers between devices: 235 us -> 72.1 us  [hop(): lax.ppermute(self.above[-1], 'col', down(self.n, distance))]
    pallas_call x0 -> x1, Pallas kernels: none -> 138 us  [substitute(): pl.pallas_call(functools.partial(substitute_kernel, rows_n), out_shape=(j...]
    ppermute x15 -> x6, waiting for transfers between devices: 103 us -> 0.02 us  [hop(): self.below.append(lax.ppermute(self.below[-1], 'col', up(self.n, distance)))]
    ppermute x0 -> x15, waiting for transfers between devices: none -> 83.7 us  [the longest x6 48.9 us: hop(): lax.ppermute(u.astype(jnp.bfloat16), 'col', [(z, z + 1) for z in range(se...]
    all_gather x8 -> x2, waiting for transfers between devices: 0.03 us -> 74.9 us  [the longest x1 41.9 us: shards(): head = lax.all_gather(head, 'col', axis=3, tiled=True)]
    ppermute x0 -> x15, starting transfers between devices: none -> 56.1 us  [the longest x6 45.1 us: hop(): lax.ppermute(u.astype(jnp.bfloat16), 'col', [(z, z + 1) for z in range(se...]
    ppermute x15 -> x6, starting transfers between devices: 30.6 us -> 7.7 us  [hop(): lax.ppermute(self.above[-1], 'col', down(self.n, distance))]
    dynamic_slice x9 -> x1, local copies, waits for them, and re-layouts: 21.7 us -> 1.18 us  [shards(): lax.dynamic_slice_in_dim(stacked, target * panel + r * share, share, axis=1)]
  transfers between devices with their start and end apart: 38 -> 29, of which waited for: 17 -> 12; matrix products, arithmetic and copies ran while one was open for 23% -> 17% of each run, Pallas kernels for 0% -> 22%
where the time goes in v2:
time: 627 us; the launch traced here: 619 us
  waiting for transfers between devices  231 us (37%)
  Pallas kernels  138 us (22%)
  starting transfers between devices  83 us (13%)
  matrix products  81.2 us (13%)
  local copies, waits for them, and re-layouts  43.5 us (7%)
  other arithmetic  27.7 us (4%)
  between operations  15 us (2%)
    pallas_call x1, Pallas kernels, substitute(): pl.pallas_call(functools.partial(substitute_kernel, rows_n), out_shape=(j...  138 us
    dot_general x16, matrix products, dot(): return jnp.dot(a, b, preferred_element_type=jnp.float32)  81.2 us
    ppermute x6, waiting for transfers between devices, hop(): lax.ppermute(self.above[-1], 'col', down(self.n, distance))  72.1 us
    ppermute x6, waiting for transfers between devices, hop(): lax.ppermute(u.astype(jnp.bfloat16), 'col', [(z, z + 1) for z in range(se...  48.9 us
    ppermute x6, starting transfers between devices, hop(): lax.ppermute(u.astype(jnp.bfloat16), 'col', [(z, z + 1) for z in range(se...  45.1 us
    all_gather x1, waiting for transfers between devices, shards(): head = lax.all_gather(head, 'col', axis=3, tiled=True)  41.9 us
    all_gather x1, waiting for transfers between devices, shards(): lax.all_gather(jnp.concatenate(pieces, axis=2), 'row', axis=1, tiled=True)  32.9 us
    ppermute x3, waiting for transfers between devices, shards(): lax.ppermute(piece, 'col', [(s, (s - d) % n) for s in range(n)])  22 us
  transfers between devices with their start and end apart: 29, of which 12 were waited for; matrix products, arithmetic and copies ran while one was open for 17% of the time, Pallas kernels for 22%

profile of v2, /device:TPU:0, one launch (start us, length us, event | category | flops | bytes accessed | tf_op | source)
XLA Modules:
  0.0 618.7 jit_solution(1771034589269143387)
XLA Ops:
  21.0 41.9 %all-gather.3.cloned.1.call-done.head_ref = bf16[3,3,128,1024]{3,2,1,0:T(8,128)(2,1)} async-done(((bf16[3,3,128,256]{3,2,1,0:T(8,128)(2,1)}), bf16[3,3,128,1024]{3,2,1,0:T(8,128)(2,1)}) %all-gather.3.cloned.1.call-update) | async-done | bytes 2359312 | tf_op jit(solution)/shard_map/all_gather | solution.py:176
  71.5 5.9 collective-permute-start
  80.7 137.5 %shard_map.50 = (f32[4,128,1024]{2,1,0:T(8,128)S(1)}, bf16[4,1024,1024]{2,1,0:T(8,128)(2,1)}) custom-call(f32[4,128,1024]{2,1,0:T(8,128)S(1)} %copy-done, bf16[3,3,128,1024]{3,2,1,0:T(8,128)(2,1)S(1)} %copy-done.1, bf16[4,128,1024]{2,1,0:T(8,128)(2,1)S(1)} %copy-done.2), custom_call_target="tpu_custom_call" | custom-call | flops 120000002129920 | bytes 16777216 | tf_op jit(solution)/shard_map/pallas_call | solution.py:147
  222.2 12.9 %collective-permute-done.8 = bf16[4,32,1024]{2,1,0:T(8,128)(2,1)S(1)} collective-permute-done((bf16[4,32,1024]{2,1,0:T(8,128)(2,1)S(1)}, bf16[4,32,1024]{2,1,0:T(8,128)(2,1)S(1)}, u32[]{:S(2)}, u32[]{:S(2)}) %collective-permute-start.8) | collective-permute-done | bytes 262176 | tf_op jit(solution)/shard_map/ppermute | solution.py:200
  235.1 9.1 %collective-permute-done.9 = bf16[4,32,1024]{2,1,0:T(8,128)(2,1)S(1)} collective-permute-done((bf16[4,32,1024]{2,1,0:T(8,128)(2,1)S(1)}, bf16[4,32,1024]{2,1,0:T(8,128)(2,1)S(1)}, u32[]{:S(2)}, u32[]{:S(2)}) %collective-permute-start.9) | collective-permute-done | bytes 262176 | tf_op jit(solution)/shard_map/ppermute | solution.py:200
  256.7 32.9 %all-gather.5.cloned.1.call-done = bf16[4,256,3072]{2,1,0:T(8,128)(2,1)} async-done(((bf16[4,32,3072]{2,1,0:T(8,128)(2,1)}), bf16[4,256,3072]{2,1,0:T(8,128)(2,1)}) %all-gather.5.cloned.1.call-update) | async-done | bytes 6291472 | tf_op jit(solution)/shard_map/all_gather | solution.py:201
  289.7 6.0 bitcast_convert_fusion.1
  315.1 38.1 %collective-permute-done.5 = bf16[1152,1024]{1,0:T(8,128)(2,1)} collective-permute-done((bf16[1152,1024]{1,0:T(8,128)(2,1)}, bf16[1152,1024]{1,0:T(8,128)(2,1)}, u32[]{:S(2)}, u32[]{:S(2)}) %collective-permute-start.5) | collective-permute-done | bytes 2359328 | tf_op jit(solution)/shard_map/ppermute | solution.py:37
  362.3 6.5 %constant_dynamic-slice_fusion = (bf16[4,256,1024]{2,1,0:T(8,128)(2,1)S(1)}, bf16[4,256,1024]{2,1,0:T(8,128)(2,1)}, bf16[4,256,1024]{2,1,0:T(8,128)(2,1)}, bf16[4,256,1024]{2,1,0:T(8,128)(2,1)S(1)}) fusion(bf16[4,1024,1024]{2,1,0:T(8,128)(2,1)} %get-tuple-element.37, s32[]{:T(128)S(6)} %select_n.103, s32[]{:T(128)S(6)} %select_n.99, s32[]{:T(128)S(6)} %select_n.95, ...), kind=kLoop, calls=%fused_computation.65 | loop fusion | bytes 16777232 | tf_op jit(solution)/shard_map/dynamic_slice | solution.py:192
  368.8 15.5 %collective-permute-done.11 = bf16[640,1024]{0,1:T(8,128)(2,1)} collective-permute-done((bf16[640,1024]{0,1:T(8,128)(2,1)}, bf16[640,1024]{0,1:T(8,128)(2,1)}, u32[]{:S(2)}, u32[]{:S(2)}) %collective-permute-start.11) | collective-permute-done | bytes 1310752 | tf_op jit(solution)/shard_map/ppermute | solution.py:66
  411.0 9.8 %collective-permute-done.19 = bf16[640,1024]{0,1:T(8,128)(2,1)S(1)} collective-permute-done((bf16[640,1024]{0,1:T(8,128)(2,1)S(1)}, bf16[640,1024]{0,1:T(8,128)(2,1)S(1)}, u32[]{:S(2)}, u32[]{:S(2)}) %collective-permute-start.19) | collective-permute-done | bytes 1310752 | tf_op jit(solution)/shard_map/ppermute | solution.py:66
  429.9 22.4 %collective-permute-start.21 = (bf16[640,1024]{0,1:T(8,128)(2,1)}, bf16[640,1024]{0,1:T(8,128)(2,1)S(1)}, u32[]{:S(2)}, u32[]{:S(2)}) collective-permute-start(bf16[640,1024]{0,1:T(8,128)(2,1)} %get-tuple-element.74), channel_id=1, source_target_pairs={{0,1},{1,2},{4,5},{5,6},{8,9},{9,10},{12,13},{13,14},{16,17},{17,1... | collective-permute-start | bytes 3932168 | tf_op jit(solution)/shard_map/ppermute | solution.py:66
  452.3 6.0 fusion.22
  458.4 6.1 fusion.17
  464.4 13.4 %collective-permute-done.21 = bf16[640,1024]{0,1:T(8,128)(2,1)S(1)} collective-permute-done((bf16[640,1024]{0,1:T(8,128)(2,1)}, bf16[640,1024]{0,1:T(8,128)(2,1)S(1)}, u32[]{:S(2)}, u32[]{:S(2)}) %collective-permute-start.21) | collective-permute-done | bytes 1310752 | tf_op jit(solution)/shard_map/ppermute | solution.py:66
  477.9 34.0 %collective-permute-done.18 = bf16[1152,1024]{1,0:T(8,128)(2,1)S(1)} collective-permute-done((bf16[1152,1024]{1,0:T(8,128)(2,1)}, bf16[1152,1024]{1,0:T(8,128)(2,1)S(1)}, u32[]{:S(2)}, u32[]{:S(2)}) %collective-permute-start.18) | collective-permute-done | bytes 2359328 | tf_op jit(solution)/shard_map/ppermute | solution.py:37
  513.2 6.0 fusion.24
  519.2 6.1 fusion.19
  542.5 8.2 %fusion.2 = f32[1152,1024]{1,0:T(8,128)} fusion(f32[1152,1024]{1,0:T(8,128)} %fusion.17, f32[1152,1024]{1,0:T(8,128)} %fusion.19, f32[1152,1024]{1,0:T(8,128)S(1)} %fusion.48, f32[9,128,1024]{2,1,0:T(8,128)S(1)} %get-tuple-element.59, bf16[1024,1024]{1,0:T(8,128)(2,1)S(1)} %bitcast.102, bf16[1152,1024]{1,0:T(8,128)(2,1)} %copy-done.11, ...), kind=kOutput, calls=%fused_computation.4 | convolution fusion | flops 2421817344 | bytes 30408704 | tf_op jit(solution)/shard_map/dot_general | solution.py:16
  550.7 8.3 %fusion.5 = f32[1152,1024]{1,0:T(8,128)} fusion(f32[1152,1024]{1,0:T(8,128)} %fusion.22, f32[1152,1024]{1,0:T(8,128)} %fusion.24, f32[1152,1024]{1,0:T(8,128)S(1)} %fusion.47, f32[9,128,1024]{2,1,0:T(8,128)S(1)} %get-tuple-element.58, bf16[1024,1024]{1,0:T(8,128)(2,1)S(1)} %bitcast.103, bf16[1152,1024]{1,0:T(8,128)(2,1)} %copy-done.10, ...), kind=kOutput, calls=%fused_computation.8 | convolution fusion | flops 2421817344 | bytes 30408704 | tf_op jit(solution)/shard_map/dot_general | solution.py:16
  559.1 6.0 collective-permute-done.24
  572.0 10.2 %collective-permute-done.25 = bf16[640,1024]{0,1:T(8,128)(2,1)} collective-permute-done((bf16[640,1024]{0,1:T(8,128)(2,1)}, bf16[640,1024]{0,1:T(8,128)(2,1)}, u32[]{:S(2)}, u32[]{:S(2)}) %collective-permute-start.25) | collective-permute-done | bytes 1310752 | tf_op jit(solution)/shard_map/ppermute | solution.py:66
  582.2 6.8 %collective-permute-done.26 = bf16[640,1024]{0,1:T(8,128)(2,1)} collective-permute-done((bf16[640,1024]{0,1:T(8,128)(2,1)}, bf16[640,1024]{0,1:T(8,128)(2,1)}, u32[]{:S(2)}, u32[]{:S(2)}) %collective-permute-start.26) | collective-permute-done | bytes 1310752 | tf_op jit(solution)/shard_map/ppermute | solution.py:67
  602.1 7.9 %pad_maximum_fusion = f32[28,128,1024]{2,1,0:T(8,128)} fusion(f32[5,128,1024]{2,1,0:T(8,128)S(1)} %get-tuple-element.61, f32[5,128,1024]{2,1,0:T(8,128)S(1)} %get-tuple-element.60, f32[9,128,1024]{2,1,0:T(8,128)S(1)} %bitcast.106, f32[9,128,1024]{2,1,0:T(8,128)} %bitcast.107), kind=kLoop, calls=%fused_computation | loop fusion | flops 11010048 | bytes 29360128 | tf_op jit(solution)/shard_map/concatenate | solution.py:234
  (118 shorter events, 146.0 us)
Async XLA Ops:
  7.2 55.8 %all-gather.3.cloned.1.call-start = ((), (), s32[]{:S(2)}) async-start(), calls=%async_computation | async-start | bytes 2949120 | tf_op jit(solution)/shard_map/all_gather | solution.py:176
  9.5 280.1 %all-gather.5.cloned.1.call-start = ((), (), s32[]{:S(2)}) async-start(), calls=%async_computation.1 | async-start | bytes 7077888 | tf_op jit(solution)/shard_map/all_gather | solution.py:201
  63.0 155.3 %collective-permute-start.3 = (bf16[1152,1024]{1,0:T(8,128)(2,1)}, bf16[1152,1024]{1,0:T(8,128)(2,1)}, u32[]{:S(2)}, u32[]{:S(2)}) collective-permute-start(bf16[1152,1024]{1,0:T(8,128)(2,1)} %bitcast.117), channel_id=1, source_target_pairs={{1,0},{2,1},{3,2},{5,4},{6,5},{7,6},{9,8},{10,9},{11,10},{13,12},{... | collective-permute-start | bytes 7077896 | tf_op jit(solution)/shard_map/ppermute | solution.py:37
  64.3 154.0 %collective-permute-start.2 = (bf16[1152,1024]{1,0:T(8,128)(2,1)}, bf16[1152,1024]{1,0:T(8,128)(2,1)}, u32[]{:S(2)}, u32[]{:S(2)}) collective-permute-start(bf16[1152,1024]{1,0:T(8,128)(2,1)} %bitcast.118), channel_id=1, source_target_pairs={{0,1},{1,2},{2,3},{4,5},{5,6},{6,7},{8,9},{9,10},{10,11},{12,13},{... | collective-permute-start | bytes 7077896 | tf_op jit(solution)/shard_map/ppermute | solution.py:36
  70.2 148.0 %collective-permute-start.1 = (bf16[1152,1024]{1,0:T(8,128)(2,1)}, bf16[1152,1024]{1,0:T(8,128)(2,1)}, u32[]{:S(2)}, u32[]{:S(2)}) collective-permute-start(bf16[1152,1024]{1,0:T(8,128)(2,1)} %bitcast.114), channel_id=1, source_target_pairs={{1,0},{2,1},{3,2},{5,4},{6,5},{7,6},{9,8},{10,9},{11,10},{13,12},{... | collective-permute-start | bytes 7077896 | tf_op jit(solution)/shard_map/ppermute | solution.py:37
  71.5 146.8 %collective-permute-start = (bf16[1152,1024]{1,0:T(8,128)(2,1)}, bf16[1152,1024]{1,0:T(8,128)(2,1)}, u32[]{:S(2)}, u32[]{:S(2)}) collective-permute-start(bf16[1152,1024]{1,0:T(8,128)(2,1)} %bitcast.115), channel_id=1, source_target_pairs={{0,1},{1,2},{2,3},{4,5},{5,6},{6,7},{8,9},{9,10},{10,11},{12,13},{... | collective-permute-start | bytes 7077896 | tf_op jit(solution)/shard_map/ppermute | solution.py:36
  245.1 66.5 %collective-permute-start.6 = (bf16[1152,1024]{1,0:T(8,128)(2,1)}, bf16[1152,1024]{1,0:T(8,128)(2,1)}, u32[]{:S(2)}, u32[]{:S(2)}) collective-permute-start(bf16[1152,1024]{1,0:T(8,128)(2,1)} %collective-permute-done.2), channel_id=1, source_target_pairs={{1,2},{2,3},{5,6},{6,7},{9,10},{10,11},{13,14},{14,15},{17,18},{18... | collective-permute-start | bytes 7077896 | tf_op jit(solution)/shard_map/ppermute | solution.py:36
  247.2 66.1 %collective-permute-start.7 = (bf16[1152,1024]{1,0:T(8,128)(2,1)}, bf16[1152,1024]{1,0:T(8,128)(2,1)}, u32[]{:S(2)}, u32[]{:S(2)}) collective-permute-start(bf16[1152,1024]{1,0:T(8,128)(2,1)} %collective-permute-done.3), channel_id=1, source_target_pairs={{1,0},{2,1},{5,4},{6,5},{9,8},{10,9},{13,12},{14,13},{17,16},{18,1... | collective-permute-start | bytes 7077896 | tf_op jit(solution)/shard_map/ppermute | solution.py:37
  248.5 104.7 %collective-permute-start.5 = (bf16[1152,1024]{1,0:T(8,128)(2,1)}, bf16[1152,1024]{1,0:T(8,128)(2,1)}, u32[]{:S(2)}, u32[]{:S(2)}) collective-permute-start(bf16[1152,1024]{1,0:T(8,128)(2,1)} %collective-permute-done.1), channel_id=1, source_target_pairs={{1,0},{2,1},{5,4},{6,5},{9,8},{10,9},{13,12},{14,13},{17,16},{18,1... | collective-permute-start | bytes 7077896 | tf_op jit(solution)/shard_map/ppermute | solution.py:37
  254.7 114.1 %collective-permute-start.4 = (bf16[1152,1024]{1,0:T(8,128)(2,1)}, bf16[1152,1024]{1,0:T(8,128)(2,1)}, u32[]{:S(2)}, u32[]{:S(2)}) collective-permute-start(bf16[1152,1024]{1,0:T(8,128)(2,1)} %collective-permute-done), channel_id=1, source_target_pairs={{1,2},{2,3},{5,6},{6,7},{9,10},{10,11},{13,14},{14,15},{17,18},{18... | collective-permute-start | bytes 7077896 | tf_op jit(solution)/shard_map/ppermute | solution.py:36
  295.7 73.1 %collective-permute-start.13 = (bf16[640,1024]{0,1:T(8,128)(2,1)}, bf16[640,1024]{0,1:T(8,128)(2,1)}, u32[]{:S(2)}, u32[]{:S(2)}) collective-permute-start(bf16[640,1024]{0,1:T(8,128)(2,1)} %get-tuple-element.81), channel_id=1, source_target_pairs={{0,1},{4,5},{8,9},{12,13},{16,17},{20,21},{24,25},{28,29}} | collective-permute-start | bytes 3932168 | tf_op jit(solution)/shard_map/ppermute | solution.py:66
  311.6 57.2 %collective-permute-start.14 = (bf16[640,1024]{0,1:T(8,128)(2,1)}, bf16[640,1024]{0,1:T(8,128)(2,1)}, u32[]{:S(2)}, u32[]{:S(2)}) collective-permute-start(bf16[640,1024]{0,1:T(8,128)(2,1)} %get-tuple-element.83), channel_id=1, source_target_pairs={{3,2},{7,6},{11,10},{15,14},{19,18},{23,22},{27,26},{31,30}} | collective-permute-start | bytes 3932168 | tf_op jit(solution)/shard_map/ppermute | solution.py:67
  313.3 55.5 %collective-permute-start.12 = (bf16[640,1024]{0,1:T(8,128)(2,1)}, bf16[640,1024]{0,1:T(8,128)(2,1)}, u32[]{:S(2)}, u32[]{:S(2)}) collective-permute-start(bf16[640,1024]{0,1:T(8,128)(2,1)} %get-tuple-element.79), channel_id=1, source_target_pairs={{3,2},{7,6},{11,10},{15,14},{19,18},{23,22},{27,26},{31,30}} | collective-permute-start | bytes 3932168 | tf_op jit(solution)/shard_map/ppermute | solution.py:67
  353.2 31.1 %collective-permute-start.11 = (bf16[640,1024]{0,1:T(8,128)(2,1)}, bf16[640,1024]{0,1:T(8,128)(2,1)}, u32[]{:S(2)}, u32[]{:S(2)}) collective-permute-start(bf16[640,1024]{0,1:T(8,128)(2,1)} %get-tuple-element.77), channel_id=1, source_target_pairs={{0,1},{4,5},{8,9},{12,13},{16,17},{20,21},{24,25},{28,29}} | collective-permute-start | bytes 3932168 | tf_op jit(solution)/shard_map/ppermute | solution.py:66
  389.4 31.4 %collective-permute-start.19 = (bf16[640,1024]{0,1:T(8,128)(2,1)S(1)}, bf16[640,1024]{0,1:T(8,128)(2,1)S(1)}, u32[]{:S(2)}, u32[]{:S(2)}) collective-permute-start(bf16[640,1024]{0,1:T(8,128)(2,1)S(1)} %get-tuple-element.76), channel_id=1, source_target_pairs={{0,1},{1,2},{4,5},{5,6},{8,9},{9,10},{12,13},{13,14},{16,17},{17,1... | collective-permute-start | bytes 3932168 | tf_op jit(solution)/shard_map/ppermute | solution.py:66
  406.6 71.3 %collective-permute-start.15 = (bf16[1152,1024]{1,0:T(8,128)(2,1)}, bf16[1152,1024]{1,0:T(8,128)(2,1)S(1)}, u32[]{:S(2)}, u32[]{:S(2)}) collective-permute-start(bf16[1152,1024]{1,0:T(8,128)(2,1)} %collective-permute-done.4), channel_id=1, source_target_pairs={{2,3},{6,7},{10,11},{14,15},{18,19},{22,23},{26,27},{30,31}} | collective-permute-start | bytes 7077896 | tf_op jit(solution)/shard_map/ppermute | solution.py:36
  407.6 70.3 %collective-permute-start.16 = (bf16[1152,1024]{1,0:T(8,128)(2,1)}, bf16[1152,1024]{1,0:T(8,128)(2,1)S(1)}, u32[]{:S(2)}, u32[]{:S(2)}) collective-permute-start(bf16[1152,1024]{1,0:T(8,128)(2,1)} %collective-permute-done.5), channel_id=1, source_target_pairs={{1,0},{5,4},{9,8},{13,12},{17,16},{21,20},{25,24},{29,28}} | collective-permute-start | bytes 7077896 | tf_op jit(solution)/shard_map/ppermute | solution.py:37
  408.9 69.0 %collective-permute-start.17 = (bf16[1152,1024]{1,0:T(8,128)(2,1)}, bf16[1152,1024]{1,0:T(8,128)(2,1)}, u32[]{:S(2)}, u32[]{:S(2)}) collective-permute-start(bf16[1152,1024]{1,0:T(8,128)(2,1)} %collective-permute-done.6), channel_id=1, source_target_pairs={{2,3},{6,7},{10,11},{14,15},{18,19},{22,23},{26,27},{30,31}} | collective-permute-start | bytes 7077896 | tf_op jit(solution)/shard_map/ppermute | solution.py:36
  420.8 91.1 %collective-permute-start.18 = (bf16[1152,1024]{1,0:T(8,128)(2,1)}, bf16[1152,1024]{1,0:T(8,128)(2,1)S(1)}, u32[]{:S(2)}, u32[]{:S(2)}) collective-permute-start(bf16[1152,1024]{1,0:T(8,128)(2,1)} %collective-permute-done.7), channel_id=1, source_target_pairs={{1,0},{5,4},{9,8},{13,12},{17,16},{21,20},{25,24},{29,28}} | collective-permute-start | bytes 7077896 | tf_op jit(solution)/shard_map/ppermute | solution.py:37
  429.9 48.0 %collective-permute-start.21 = (bf16[640,1024]{0,1:T(8,128)(2,1)}, bf16[640,1024]{0,1:T(8,128)(2,1)S(1)}, u32[]{:S(2)}, u32[]{:S(2)}) collective-permute-start(bf16[640,1024]{0,1:T(8,128)(2,1)} %get-tuple-element.74), channel_id=1, source_target_pairs={{0,1},{1,2},{4,5},{5,6},{8,9},{9,10},{12,13},{13,14},{16,17},{17,1... | collective-permute-start | bytes 3932168 | tf_op jit(solution)/shard_map/ppermute | solution.py:66
  526.7 32.4 %collective-permute-start.23 = (bf16[640,1024]{0,1:T(8,128)(2,1)}, bf16[640,1024]{0,1:T(8,128)(2,1)}, u32[]{:S(2)}, u32[]{:S(2)}) collective-permute-start(bf16[640,1024]{0,1:T(8,128)(2,1)} %fusion.14), channel_id=1, source_target_pairs={{0,1},{1,2},{2,3},{4,5},{5,6},{6,7},{8,9},{9,10},{10,11},{12,13},{... | collective-permute-start | bytes 3932168 | tf_op jit(solution)/shard_map/ppermute | solution.py:66
  530.9 34.2 %collective-permute-start.24 = (bf16[640,1024]{0,1:T(8,128)(2,1)}, bf16[640,1024]{0,1:T(8,128)(2,1)}, u32[]{:S(2)}, u32[]{:S(2)}) collective-permute-start(bf16[640,1024]{0,1:T(8,128)(2,1)} %fusion.15), channel_id=1, source_target_pairs={{1,0},{2,1},{3,2},{5,4},{6,5},{7,6},{9,8},{10,9},{11,10},{13,12},{... | collective-permute-start | bytes 3932168 | tf_op jit(solution)/shard_map/ppermute | solution.py:67
  533.8 48.4 %collective-permute-start.25 = (bf16[640,1024]{0,1:T(8,128)(2,1)}, bf16[640,1024]{0,1:T(8,128)(2,1)}, u32[]{:S(2)}, u32[]{:S(2)}) collective-permute-start(bf16[640,1024]{0,1:T(8,128)(2,1)} %fusion.12), channel_id=1, source_target_pairs={{0,1},{1,2},{2,3},{4,5},{5,6},{6,7},{8,9},{9,10},{10,11},{12,13},{... | collective-permute-start | bytes 3932168 | tf_op jit(solution)/shard_map/ppermute | solution.py:66
  540.9 48.1 %collective-permute-start.26 = (bf16[640,1024]{0,1:T(8,128)(2,1)}, bf16[640,1024]{0,1:T(8,128)(2,1)}, u32[]{:S(2)}, u32[]{:S(2)}) collective-permute-start(bf16[640,1024]{0,1:T(8,128)(2,1)} %fusion.13), channel_id=1, source_target_pairs={{1,0},{2,1},{3,2},{5,4},{6,5},{7,6},{9,8},{10,9},{11,10},{13,12},{... | collective-permute-start | bytes 3932168 | tf_op jit(solution)/shard_map/ppermute | solution.py:67
  (25 other events, 461.5 us)
Sparse Core Ops, SparseCore 0:
  9.7 53.2 all-gather.2
  245.2 44.4 all-gather.4

commit v3 on v2

--- a/solution.py
+++ b/solution.py
@@ -8,8 +8,8 @@
 from jax.sharding import PartitionSpec as P
 
 STEPS = 4
-GATHERED = (9, 9)
-REDUCED = (5, 5)
+GATHERED = (20,)
+REDUCED = (8,)
 
 
 def dot(a, b):

time: 627 us -> 567 us (0.904); the launches traced: 619 us -> 566 us
  starting transfers between devices: 83 us -> 41.3 us
  matrix products: 81.2 us -> 72.6 us
    ppermute x6 -> x3, starting transfers between devices: 45.1 us -> 17.2 us  [hop(): lax.ppermute(u.astype(jnp.bfloat16), 'col', [(z, z + 1) for z in range(se...]
    ppermute x6 -> x3, waiting for transfers between devices: 72.1 us -> 93.7 us  [hop(): lax.ppermute(self.above[-1], 'col', down(self.n, distance))]
    ppermute x6 -> x3, waiting for transfers between devices: 48.9 us -> 29.2 us  [hop(): lax.ppermute(u.astype(jnp.bfloat16), 'col', [(z, z + 1) for z in range(se...]
    dot_general x16 -> x8, matrix products: 81.2 us -> 72.6 us  [dot(): return jnp.dot(a, b, preferred_element_type=jnp.float32)]
    slice x2 -> x4, local copies, waits for them, and re-layouts: 7.43 us -> 0.24 us  [shards(): flat = factor[start:start + count].reshape(count * tile_rows, STEPS * panel)]
    add x2 -> x0, local copies, waits for them, and re-layouts: 6.6 us -> none  [total(): self.products[0] + self.upward.astype(jnp.float32)]
    ppermute x6 -> x3, starting transfers between devices: 19.1 us -> 12.9 us  [hop(): self.below.append(lax.ppermute(self.below[-1], 'col', up(self.n, distance)))]
    ppermute x6 -> x3, waiting for transfers between devices: 12.8 us -> 7.67 us  [hop(): lax.ppermute(v.astype(jnp.bfloat16), 'col', [(z, z - 1) for z in range(se...]
  transfers between devices with their start and end apart: 29 -> 17, of which waited for: 12 -> 9; matrix products, arithmetic and copies ran while one was open for 17% -> 17% of each run, Pallas kernels for 22% -> 24%
where the time goes in v3:
time: 567 us; the launch traced here: 566 us
  waiting for transfers between devices  237 us (42%)
  Pallas kernels  137 us (24%)
  matrix products  72.6 us (13%)
  starting transfers between devices  41.3 us (7%)
  local copies, waits for them, and re-layouts  37.5 us (7%)
  other arithmetic  26.4 us (5%)
  between operations  14.3 us (3%)
    pallas_call x1, Pallas kernels, substitute(): pl.pallas_call(functools.partial(substitute_kernel, rows_n), out_shape=(j...  137 us
    ppermute x3, waiting for transfers between devices, hop(): lax.ppermute(self.above[-1], 'col', down(self.n, distance))  93.7 us
    dot_general x8, matrix products, dot(): return jnp.dot(a, b, preferred_element_type=jnp.float32)  72.6 us
    all_gather x1, waiting for transfers between devices, shards(): head = lax.all_gather(head, 'col', axis=3, tiled=True)  45.8 us
    all_gather x1, waiting for transfers between devices, shards(): lax.all_gather(jnp.concatenate(pieces, axis=2), 'row', axis=1, tiled=True)  38.3 us
    ppermute x3, waiting for transfers between devices, hop(): lax.ppermute(u.astype(jnp.bfloat16), 'col', [(z, z + 1) for z in range(se...  29.2 us
    ppermute x3, waiting for transfers between devices, shards(): lax.ppermute(piece, 'col', [(s, (s - d) % n) for s in range(n)])  22 us
    ppermute x3, starting transfers between devices, hop(): lax.ppermute(u.astype(jnp.bfloat16), 'col', [(z, z + 1) for z in range(se...  17.2 us
  transfers between devices with their start and end apart: 17, of which 9 were waited for; matrix products, arithmetic and copies ran while one was open for 17% of the time, Pallas kernels for 24%

profile of v3, /device:TPU:0, one launch (start us, length us, event | category | flops | bytes accessed | tf_op | source)
XLA Modules:
  0.0 566.2 jit_solution(15943708274848169817)
XLA Ops:
  17.2 45.8 %all-gather.3.cloned.1.call-done.head_ref = bf16[3,3,128,1024]{3,2,1,0:T(8,128)(2,1)} async-done(((bf16[3,3,128,256]{3,2,1,0:T(8,128)(2,1)}), bf16[3,3,128,1024]{3,2,1,0:T(8,128)(2,1)}) %all-gather.3.cloned.1.call-update) | async-done | bytes 2359312 | tf_op jit(solution)/shard_map/all_gather | solution.py:176
  64.3 6.9 %collective-permute-start = (bf16[2560,1024]{1,0:T(8,128)(2,1)}, bf16[2560,1024]{1,0:T(8,128)(2,1)}, u32[]{:S(2)}, u32[]{:S(2)}) collective-permute-start(bf16[2560,1024]{1,0:T(8,128)(2,1)} %bitcast.61), channel_id=1, source_target_pairs={{0,1},{1,2},{2,3},{4,5},{5,6},{6,7},{8,9},{9,10},{10,11},{12,13},{... | collective-permute-start | bytes 15728648 | tf_op jit(solution)/shard_map/ppermute | solution.py:36
  74.4 137.4 %shard_map.50 = (f32[4,128,1024]{2,1,0:T(8,128)S(1)}, bf16[4,1024,1024]{2,1,0:T(8,128)(2,1)}) custom-call(f32[4,128,1024]{2,1,0:T(8,128)S(1)} %copy-done, bf16[3,3,128,1024]{3,2,1,0:T(8,128)(2,1)S(1)} %copy-done.1, bf16[4,128,1024]{2,1,0:T(8,128)(2,1)S(1)} %copy-done.2), custom_call_target="tpu_custom_call" | custom-call | flops 120000002129920 | bytes 16777216 | tf_op jit(solution)/shard_map/pallas_call | solution.py:147
  215.8 12.9 %collective-permute-done.4 = bf16[4,32,1024]{2,1,0:T(8,128)(2,1)S(1)} collective-permute-done((bf16[4,32,1024]{2,1,0:T(8,128)(2,1)S(1)}, bf16[4,32,1024]{2,1,0:T(8,128)(2,1)S(1)}, u32[]{:S(2)}, u32[]{:S(2)}) %collective-permute-start.4) | collective-permute-done | bytes 262176 | tf_op jit(solution)/shard_map/ppermute | solution.py:200
  228.6 9.1 %collective-permute-done.5 = bf16[4,32,1024]{2,1,0:T(8,128)(2,1)S(1)} collective-permute-done((bf16[4,32,1024]{2,1,0:T(8,128)(2,1)S(1)}, bf16[4,32,1024]{2,1,0:T(8,128)(2,1)S(1)}, u32[]{:S(2)}, u32[]{:S(2)}) %collective-permute-start.5) | collective-permute-done | bytes 262176 | tf_op jit(solution)/shard_map/ppermute | solution.py:200
  245.0 38.3 %all-gather.5.cloned.1.call-done = bf16[4,256,3072]{2,1,0:T(8,128)(2,1)} async-done(((bf16[4,32,3072]{2,1,0:T(8,128)(2,1)}), bf16[4,256,3072]{2,1,0:T(8,128)(2,1)}) %all-gather.5.cloned.1.call-update) | async-done | bytes 6291472 | tf_op jit(solution)/shard_map/all_gather | solution.py:201
  283.3 6.8 %bitcast_convert_fusion = (bf16[1024,1024]{0,1:T(8,128)(2,1)S(1)}, f32[1024,1024]{1,0:T(8,128)}) fusion(bf16[1024,1024]{1,0:T(8,128)(2,1)} %bitcast.70, bf16[1024,3072]{1,0:T(8,128)(2,1)} %bitcast.74), kind=kOutput, calls=%fused_computation.20 | convolution fusion | flops 2148532224 | bytes 10485760 | tf_op jit(solution)/shard_map/dot_general | solution.py:16
  292.0 5.9 %bitcast_convert_fusion.1 = (bf16[1024,1024]{0,1:T(8,128)(2,1)S(1)}, f32[1024,1024]{1,0:T(8,128)}) fusion(bf16[1024,1024]{1,0:T(8,128)(2,1)S(1)} %bitcast.71, bf16[1024,3072]{1,0:T(8,128)(2,1)} %bitcast.75), kind=kOutput, calls=%fused_computation.23 | convolution fusion | flops 2148532224 | bytes 10485760 | tf_op jit(solution)/shard_map/dot_general | solution.py:16
  297.9 4.8 collective-permute-start.7
  302.6 53.4 %collective-permute-done.3 = bf16[2560,1024]{1,0:T(8,128)(2,1)} collective-permute-done((bf16[2560,1024]{1,0:T(8,128)(2,1)}, bf16[2560,1024]{1,0:T(8,128)(2,1)}, u32[]{:S(2)}, u32[]{:S(2)}) %collective-permute-start.3) | collective-permute-done | bytes 5242912 | tf_op jit(solution)/shard_map/ppermute | solution.py:37
  360.7 10.0 %slice.30 = f32[20,128,1024]{2,1,0:T(8,128)} slice(f32[32,128,1024]{2,1,0:T(8,128)} %param.3), slice={[4:24], [0:128], [0:1024]} | slice | bytes 20971520 | tf_op jit(solution)/shard_map/slice | solution.py:228
  375.3 7.7 %fusion.13 = (bf16[1024,1024]{0,1:T(8,128)(2,1)}, bf16[1024,1024]{0,1:T(8,128)(2,1)}) fusion(bf16[1024,1024]{0,1:T(8,128)(2,1)} %collective-permute-done.8, bf16[1024,1024]{0,1:T(8,128)(2,1)} %collective-permute-done.7, bf16[1024,1024]{1,0:T(8,128)(2,1)S(1)} %bitcast.72, bf16[1024,3072]{1,0:T(8,128)(2,1)} %bitcast.76), kind=kOutput, calls=%fused_computation.18 | convolution fusion | flops 2153775104 | bytes 12582912 | tf_op jit(solution)/shard_map/dot_general | solution.py:16
  383.8 9.7 %collective-permute-start.11 = (bf16[1024,1024]{0,1:T(8,128)(2,1)}, bf16[1024,1024]{0,1:T(8,128)(2,1)}, u32[]{:S(2)}, u32[]{:S(2)}) collective-permute-start(bf16[1024,1024]{0,1:T(8,128)(2,1)} %get-tuple-element.40), channel_id=1, source_target_pairs={{0,1},{1,2},{4,5},{5,6},{8,9},{9,10},{12,13},{13,14},{16,17},{17,1... | collective-permute-start | bytes 6291464 | tf_op jit(solution)/shard_map/ppermute | solution.py:66
  393.5 8.1 %fusion.22 = f32[2560,1024]{1,0:T(8,128)} fusion(bf16[2560,1024]{1,0:T(8,128)(2,1)S(1)} %bitcast.64, bf16[1024,1024]{1,0:T(8,128)(2,1)S(1)} %bitcast.68), kind=kOutput, calls=%fused_computation.41 | convolution fusion | flops 5368709120 | bytes 17825792 | tf_op jit(solution)/shard_map/dot_general | solution.py:16
  404.0 10.9 %fusion.4 = f32[2560,1024]{1,0:T(8,128)} fusion(bf16[1024,1024]{1,0:T(8,128)(2,1)S(1)} %bitcast.67, bf16[2560,1024]{1,0:T(8,128)(2,1)} %collective-permute-done.3, bf16[2560,1024]{1,0:T(8,128)(2,1)} %collective-permute-done.2, pred[]{:T(512)S(6)} %lt.71), kind=kOutput, calls=%fused_computation.6 | convolution fusion | flops 5371330560 | bytes 23068672 | tf_op jit(solution)/shard_map/dot_general | solution.py:16
  414.8 21.5 %collective-permute-done.11 = bf16[1024,1024]{0,1:T(8,128)(2,1)} collective-permute-done((bf16[1024,1024]{0,1:T(8,128)(2,1)}, bf16[1024,1024]{0,1:T(8,128)(2,1)}, u32[]{:S(2)}, u32[]{:S(2)}) %collective-permute-start.11) | collective-permute-done | bytes 2097184 | tf_op jit(solution)/shard_map/ppermute | solution.py:66
  436.3 40.3 %collective-permute-done.10 = bf16[2560,1024]{1,0:T(8,128)(2,1)} collective-permute-done((bf16[2560,1024]{1,0:T(8,128)(2,1)}, bf16[2560,1024]{1,0:T(8,128)(2,1)}, u32[]{:S(2)}, u32[]{:S(2)}) %collective-permute-start.10) | collective-permute-done | bytes 5242912 | tf_op jit(solution)/shard_map/ppermute | solution.py:37
  486.9 10.7 %fusion.6 = f32[2560,1024]{1,0:T(8,128)} fusion(bf16[1024,1024]{1,0:T(8,128)(2,1)S(1)} %bitcast.66, bf16[2560,1024]{1,0:T(8,128)(2,1)} %collective-permute-done.1, bf16[2560,1024]{1,0:T(8,128)(2,1)} %collective-permute-done.9, pred[]{:T(512)S(6)} %lt.62), kind=kOutput, calls=%fused_computation.8 | convolution fusion | flops 5371330560 | bytes 23068672 | tf_op jit(solution)/shard_map/dot_general | solution.py:16
  497.6 20.3 %fusion.2 = f32[2560,1024]{1,0:T(8,128)} fusion(f32[2560,1024]{1,0:T(8,128)} %fusion.4, f32[2560,1024]{1,0:T(8,128)} %fusion.6, f32[2560,1024]{1,0:T(8,128)} %fusion.22, f32[20,128,1024]{2,1,0:T(8,128)} %slice.30, bf16[1024,1024]{1,0:T(8,128)(2,1)S(1)} %bitcast.59, bf16[2560,1024]{1,0:T(8,128)(2,1)} %collective-permute-done.10, ...), kind=kOutput, calls=%fused_computation.4 | convolution fusion | flops 5381816320 | bytes 65011712 | tf_op jit(solution)/shard_map/dot_general | solution.py:16
  517.9 7.7 %collective-permute-done.13 = bf16[1024,1024]{0,1:T(8,128)(2,1)} collective-permute-done((bf16[1024,1024]{0,1:T(8,128)(2,1)}, bf16[1024,1024]{0,1:T(8,128)(2,1)}, u32[]{:S(2)}, u32[]{:S(2)}) %collective-permute-start.13) | collective-permute-done | bytes 2097184 | tf_op jit(solution)/shard_map/ppermute | solution.py:66
  525.6 7.7 %collective-permute-done.14 = bf16[1024,1024]{0,1:T(8,128)(2,1)} collective-permute-done((bf16[1024,1024]{0,1:T(8,128)(2,1)}, bf16[1024,1024]{0,1:T(8,128)(2,1)}, u32[]{:S(2)}, u32[]{:S(2)}) %collective-permute-start.14) | collective-permute-done | bytes 2097184 | tf_op jit(solution)/shard_map/ppermute | solution.py:67
  533.2 5.4 fusion.11
  538.6 5.4 copy.9
  548.4 9.7 %pad_maximum_fusion = f32[28,128,1024]{2,1,0:T(8,128)} fusion(f32[8,128,1024]{2,1,0:T(8,128)S(1)} %slice_subtract_fusion, f32[20,128,1024]{2,1,0:T(8,128)} %bitcast.55), kind=kLoop, calls=%fused_computation | loop fusion | flops 3670016 | bytes 29360128 | tf_op jit(solution)/shard_map/concatenate | solution.py:234
  (60 shorter events, 55.9 us)
Async XLA Ops:
  7.2 55.8 %all-gather.3.cloned.1.call-start = ((), (), s32[]{:S(2)}) async-start(), calls=%async_computation | async-start | bytes 2949120 | tf_op jit(solution)/shard_map/all_gather | solution.py:176
  9.6 273.7 %all-gather.5.cloned.1.call-start = ((), (), s32[]{:S(2)}) async-start(), calls=%async_computation.1 | async-start | bytes 7077888 | tf_op jit(solution)/shard_map/all_gather | solution.py:201
  13.2 57.9 %copy-start.2 = (bf16[4,128,1024]{2,1,0:T(8,128)(2,1)S(1)}, bf16[4,128,1024]{2,1,0:T(8,128)(2,1)}, u32[]{:S(2)}) copy-start(bf16[4,128,1024]{2,1,0:T(8,128)(2,1)} %inverse_ref.1) | copy-start | bytes 3145732
  63.0 148.9 %collective-permute-start.1 = (bf16[2560,1024]{1,0:T(8,128)(2,1)}, bf16[2560,1024]{1,0:T(8,128)(2,1)}, u32[]{:S(2)}, u32[]{:S(2)}) collective-permute-start(bf16[2560,1024]{1,0:T(8,128)(2,1)} %bitcast.60), channel_id=1, source_target_pairs={{1,0},{2,1},{3,2},{5,4},{6,5},{7,6},{9,8},{10,9},{11,10},{13,12},{... | collective-permute-start | bytes 15728648 | tf_op jit(solution)/shard_map/ppermute | solution.py:37
  64.3 147.6 %collective-permute-start = (bf16[2560,1024]{1,0:T(8,128)(2,1)}, bf16[2560,1024]{1,0:T(8,128)(2,1)}, u32[]{:S(2)}, u32[]{:S(2)}) collective-permute-start(bf16[2560,1024]{1,0:T(8,128)(2,1)} %bitcast.61), channel_id=1, source_target_pairs={{0,1},{1,2},{2,3},{4,5},{5,6},{6,7},{8,9},{9,10},{10,11},{12,13},{... | collective-permute-start | bytes 15728648 | tf_op jit(solution)/shard_map/ppermute | solution.py:36
  213.0 15.6 %collective-permute-start.4 = (bf16[4,32,1024]{2,1,0:T(8,128)(2,1)S(1)}, bf16[4,32,1024]{2,1,0:T(8,128)(2,1)S(1)}, u32[]{:S(2)}, u32[]{:S(2)}) collective-permute-start(bf16[4,32,1024]{2,1,0:T(8,128)(2,1)S(1)} %get-tuple-element.36), channel_id=1, source_target_pairs={{0,3},{1,0},{2,1},{3,2},{4,7},{5,4},{6,5},{7,6},{8,11},{9,8},{10,9... | collective-permute-start | bytes 786440 | tf_op jit(solution)/shard_map/ppermute | solution.py:200
  213.1 15.6 %collective-permute-start.6 = (bf16[4,32,1024]{2,1,0:T(8,128)(2,1)S(1)}, bf16[4,32,1024]{2,1,0:T(8,128)(2,1)S(1)}, u32[]{:S(2)}, u32[]{:S(2)}) collective-permute-start(bf16[4,32,1024]{2,1,0:T(8,128)(2,1)S(1)} %get-tuple-element.37), channel_id=1, source_target_pairs={{0,1},{1,2},{2,3},{3,0},{4,5},{5,6},{6,7},{7,4},{8,9},{9,10},{10,1... | collective-permute-start | bytes 786440 | tf_op jit(solution)/shard_map/ppermute | solution.py:200
  215.1 22.6 %collective-permute-start.5 = (bf16[4,32,1024]{2,1,0:T(8,128)(2,1)S(1)}, bf16[4,32,1024]{2,1,0:T(8,128)(2,1)S(1)}, u32[]{:S(2)}, u32[]{:S(2)}) collective-permute-start(bf16[4,32,1024]{2,1,0:T(8,128)(2,1)S(1)} %get-tuple-element.38), channel_id=1, source_target_pairs={{0,2},{1,3},{2,0},{3,1},{4,6},{5,7},{6,4},{7,5},{8,10},{9,11},{10,... | collective-permute-start | bytes 786440 | tf_op jit(solution)/shard_map/ppermute | solution.py:200
  238.7 117.3 %collective-permute-start.3 = (bf16[2560,1024]{1,0:T(8,128)(2,1)}, bf16[2560,1024]{1,0:T(8,128)(2,1)}, u32[]{:S(2)}, u32[]{:S(2)}) collective-permute-start(bf16[2560,1024]{1,0:T(8,128)(2,1)} %collective-permute-done.1), channel_id=1, source_target_pairs={{1,0},{2,1},{5,4},{6,5},{9,8},{10,9},{13,12},{14,13},{17,16},{18,1... | collective-permute-start | bytes 15728648 | tf_op jit(solution)/shard_map/ppermute | solution.py:37
  240.2 115.9 %collective-permute-start.2 = (bf16[2560,1024]{1,0:T(8,128)(2,1)}, bf16[2560,1024]{1,0:T(8,128)(2,1)}, u32[]{:S(2)}, u32[]{:S(2)}) collective-permute-start(bf16[2560,1024]{1,0:T(8,128)(2,1)} %collective-permute-done), channel_id=1, source_target_pairs={{1,2},{2,3},{5,6},{6,7},{9,10},{10,11},{13,14},{14,15},{17,18},{18... | collective-permute-start | bytes 15728648 | tf_op jit(solution)/shard_map/ppermute | solution.py:36
  283.3 8.7 %copy-start.5 = (bf16[128,8,4,256]{3,1,2,0:T(8,128)(2,1)S(1)}, bf16[128,8,4,256]{3,1,2,0:T(8,128)(2,1)}, u32[]{:S(2)}) copy-start(bf16[128,8,4,256]{3,1,2,0:T(8,128)(2,1)} %copy.12) | copy-start | bytes 6291460
  290.0 66.0 %collective-permute-start.8 = (bf16[1024,1024]{0,1:T(8,128)(2,1)S(1)}, bf16[1024,1024]{0,1:T(8,128)(2,1)}, u32[]{:S(2)}, u32[]{:S(2)}) collective-permute-start(bf16[1024,1024]{0,1:T(8,128)(2,1)S(1)} %get-tuple-element.43), channel_id=1, source_target_pairs={{3,2},{7,6},{11,10},{15,14},{19,18},{23,22},{27,26},{31,30}} | collective-permute-start | bytes 6291464 | tf_op jit(solution)/shard_map/ppermute | solution.py:67
  297.9 58.2 %collective-permute-start.7 = (bf16[1024,1024]{0,1:T(8,128)(2,1)S(1)}, bf16[1024,1024]{0,1:T(8,128)(2,1)}, u32[]{:S(2)}, u32[]{:S(2)}) collective-permute-start(bf16[1024,1024]{0,1:T(8,128)(2,1)S(1)} %get-tuple-element.41), channel_id=1, source_target_pairs={{0,1},{4,5},{8,9},{12,13},{16,17},{20,21},{24,25},{28,29}} | collective-permute-start | bytes 6291464 | tf_op jit(solution)/shard_map/ppermute | solution.py:66
  356.1 80.3 %collective-permute-start.9 = (bf16[2560,1024]{1,0:T(8,128)(2,1)}, bf16[2560,1024]{1,0:T(8,128)(2,1)}, u32[]{:S(2)}, u32[]{:S(2)}) collective-permute-start(bf16[2560,1024]{1,0:T(8,128)(2,1)} %collective-permute-done.2), channel_id=1, source_target_pairs={{2,3},{6,7},{10,11},{14,15},{18,19},{22,23},{26,27},{30,31}} | collective-permute-start | bytes 15728648 | tf_op jit(solution)/shard_map/ppermute | solution.py:36
  359.1 117.5 %collective-permute-start.10 = (bf16[2560,1024]{1,0:T(8,128)(2,1)}, bf16[2560,1024]{1,0:T(8,128)(2,1)}, u32[]{:S(2)}, u32[]{:S(2)}) collective-permute-start(bf16[2560,1024]{1,0:T(8,128)(2,1)} %collective-permute-done.3), channel_id=1, source_target_pairs={{1,0},{5,4},{9,8},{13,12},{17,16},{21,20},{25,24},{29,28}} | collective-permute-start | bytes 15728648 | tf_op jit(solution)/shard_map/ppermute | solution.py:37
  370.7 4.6 copy-start.6
  370.7 22.8 %slice-start.2 = ((s8[5242880]{0:T(1024)(128)(4,1)}), s8[1048576]{0:T(1024)(128)(4,1)S(1)}, s32[]{:S(2)}) async-start(s8[5242880]{0:T(1024)(128)(4,1)} %bitcast.62), calls=%async_computation.4 | async-start | bytes 2097152
  375.3 18.1 %slice-start.3 = ((s8[5242880]{0:T(1024)(128)(4,1)}), s8[4194304]{0:T(1024)(128)(4,1)S(1)}, s32[]{:S(2)}) async-start(s8[5242880]{0:T(1024)(128)(4,1)} %bitcast.62), calls=%async_computation.5 | async-start | bytes 8388608
  383.0 31.8 %collective-permute-start.12 = (bf16[1024,1024]{0,1:T(8,128)(2,1)}, bf16[1024,1024]{0,1:T(8,128)(2,1)S(1)}, u32[]{:S(2)}, u32[]{:S(2)}) collective-permute-start(bf16[1024,1024]{0,1:T(8,128)(2,1)} %get-tuple-element.39), channel_id=1, source_target_pairs={{2,1},{3,2},{6,5},{7,6},{10,9},{11,10},{14,13},{15,14},{18,17},{19... | collective-permute-start | bytes 6291464 | tf_op jit(solution)/shard_map/ppermute | solution.py:67
  383.8 52.5 %collective-permute-start.11 = (bf16[1024,1024]{0,1:T(8,128)(2,1)}, bf16[1024,1024]{0,1:T(8,128)(2,1)}, u32[]{:S(2)}, u32[]{:S(2)}) collective-permute-start(bf16[1024,1024]{0,1:T(8,128)(2,1)} %get-tuple-element.40), channel_id=1, source_target_pairs={{0,1},{1,2},{4,5},{5,6},{8,9},{9,10},{12,13},{13,14},{16,17},{17,1... | collective-permute-start | bytes 6291464 | tf_op jit(solution)/shard_map/ppermute | solution.py:66
  404.0 72.7 %copy-start.4 = (f32[1024,1024]{1,0:T(8,128)S(1)}, f32[1024,1024]{1,0:T(8,128)}, u32[]{:S(2)}) copy-start(f32[1024,1024]{1,0:T(8,128)} %get-tuple-element.44) | copy-start | bytes 12582916
  414.8 68.4 %copy-start.3 = (f32[1024,1024]{1,0:T(8,128)S(1)}, f32[1024,1024]{1,0:T(8,128)}, u32[]{:S(2)}) copy-start(f32[1024,1024]{1,0:T(8,128)} %get-tuple-element.42) | copy-start | bytes 12582916
  480.4 45.2 %collective-permute-start.13 = (bf16[1024,1024]{0,1:T(8,128)(2,1)}, bf16[1024,1024]{0,1:T(8,128)(2,1)}, u32[]{:S(2)}, u32[]{:S(2)}) collective-permute-start(bf16[1024,1024]{0,1:T(8,128)(2,1)} %fusion.14), channel_id=1, source_target_pairs={{0,1},{1,2},{2,3},{4,5},{5,6},{6,7},{8,9},{9,10},{10,11},{12,13},{... | collective-permute-start | bytes 6291464 | tf_op jit(solution)/shard_map/ppermute | solution.py:66
  485.4 47.8 %collective-permute-start.14 = (bf16[1024,1024]{0,1:T(8,128)(2,1)}, bf16[1024,1024]{0,1:T(8,128)(2,1)}, u32[]{:S(2)}, u32[]{:S(2)}) collective-permute-start(bf16[1024,1024]{0,1:T(8,128)(2,1)} %fusion.15), channel_id=1, source_target_pairs={{1,0},{2,1},{3,2},{5,4},{6,5},{7,6},{9,8},{10,9},{11,10},{13,12},{... | collective-permute-start | bytes 6291464 | tf_op jit(solution)/shard_map/ppermute | solution.py:67
  (4 other events, 11.2 us)
Sparse Core Ops, SparseCore 0:
  9.7 53.2 all-gather.2
  238.8 44.3 all-gather.4
